TPU v7x, 32 devices: a whole 2x2x4 slice. The times are simulated.
32 devices in a mesh: region: 4 (over y, x), tile: 8 (over z, core).
Axes of the slice: x: 2, y: 2, z: 4, core: 2. Of those that a mesh axis runs over, the one named last changes fastest.
Arguments:
- right_side: float32 [16, 32, 32, 256], P('region', 'tile'), may hold values from -20 to 20
- coords: float32 [16, 32, 2, 256], P('region', 'tile'), may hold values from 0 to 1
- pair_list: int32 [8, 16, 32], P(None, 'region', 'tile'), may hold values from 0 to 1, as said below
Outputs:
- solution: float32 [16, 32, 32, 256], P('region', 'tile')
- residual: float32 [16, 32, 32, 256], P('region', 'tile')
Inputs may be any that keep to these rules, and one draw needn't show every extreme that they name: pair_list[k + 4] at a block equals pair_list[k] at its neighbour in direction k + 4, for k < 4; a direction that leaves the grid of 16 x 32 blocks is 0.
All inputs are finite; a program needn't handle non-finite values.
Results may differ from a plain program's by a relative error of at most 0.0003.
Values sent between devices are 32-bit elements; how exact they have to be, the bound alone decides.
No kernel may reach another device: no remote copies, remote signals or barrier semaphores. Data moves between devices by JAX's collectives and lax.ppermute only.
A program may use at most 64 MiB of HBM per device.

v0:
```python
import functools

import jax
import jax.numpy as jnp
from jax import lax
from jax.experimental import pallas as pl
from jax.experimental.pallas import tpu as pltpu
from jax.sharding import PartitionSpec as P

LENGTH_SCALE = 0.2
TAPER_RANGE = 0.5
NUGGET = 3.0
OFFSETS = ((0, 1), (1, 0), (1, 1), (1, -1), (0, -1), (-1, 0), (-1, -1), (-1, 1))
UNIT = 1.4426950408889634 / LENGTH_SCALE
EDGE = UNIT * TAPER_RANGE
WEIGHT = 4.0 * 2.0**-EDGE / EDGE**5
STRIP = 64
LONG_TURN_LOG2 = 3
VMEM_LIMIT = 10 * 1024 * 1024


def dot_nn(a, b):
    return lax.dot_general(a, b, (((1,), (0,)), ((), ())), preferred_element_type=jnp.float32)


def dot_nt(a, b):
    return lax.dot_general(a, b, (((1,), (1,)), ((), ())), preferred_element_type=jnp.float32)


def split_hi_lo(values):
    hi = values.astype(jnp.bfloat16)
    lo = (values - hi.astype(jnp.float32)).astype(jnp.bfloat16)
    return hi, lo


def across_lanes(row, lanes):
    return jnp.transpose(jnp.broadcast_to(row, (lanes, row.shape[1])))


def make_tile(keep_ref, slot, spread_ref, down, points_ref, along, shift_a, shift_b):
    points = keep_ref.shape[2]
    lanes = spread_ref.shape[3]
    row_x = points_ref[along, 0:1] - shift_a
    row_y = points_ref[along, 1:2] - shift_b
    for start in range(0, points, STRIP):
        rows = slice(start, start + STRIP)
        for left in range(0, points, lanes):
            cols = slice(left, left + lanes)
            gap_x = spread_ref[down, 0, rows] - row_x[:, cols]
            gap_y = spread_ref[down, 1, rows] - row_y[:, cols]
            square = jnp.maximum(gap_x * gap_x + gap_y * gap_y, 1e-30)
            rest = jnp.maximum(EDGE - square * lax.rsqrt(square), 0.0)
            rest2 = rest * rest
            cov = (jnp.exp2(rest) * (rest2 * rest2)) * (1.25 * EDGE - rest)
            for part, values in enumerate(split_hi_lo(cov)):
                keep_ref[slot, part, rows, cols] = values


def product(dot, parts_ref, at, high, low):
    rhs = parts_ref.shape[1] // 2
    both = dot(parts_ref[at], high)
    cross = dot(parts_ref[at, 0:rhs], low)
    return both[:rhs] + both[rhs:] + cross


def store_parts(parts_ref, at, values):
    rhs = values.shape[0]
    hi, lo = split_hi_lo(values * WEIGHT)
    parts_ref[at, 0:rhs] = hi
    parts_ref[at, rhs : 2 * rhs] = lo


def in_turns(count, step):
    turns = lax.shift_right_logical(count + 1, 1)

    def one_turn(turn, carry):
        step(2 * turn)
        step(2 * turn + 1)
        return carry

    lax.fori_loop(0, turns, one_turn, 0)


def only_use(first, last, kept_ref, use):
    def one_turn(start, length):
        for n in range(length):
            use(kept_ref[start + n, 0], kept_ref[start + n, 1], start + n)

    whole = lax.shift_right_logical(last - first, LONG_TURN_LOG2)
    lax.fori_loop(0, whole, lambda turn, c: (one_turn(first + (turn << LONG_TURN_LOG2), 1 << LONG_TURN_LOG2), c)[1], 0)
    lax.fori_loop(first + (whole << LONG_TURN_LOG2), last, lambda n, c: (one_turn(n, 1), c)[1], 0)


def item_code(own, other, shift_a, shift_b):
    return own + 64 * other + 4096 * (shift_a + 1) + 16384 * (shift_b + 1)


NO_ITEM = item_code(0, 0, 2, 2)


def item_blocks(code):
    return lax.bitwise_and(code, 63), lax.bitwise_and(lax.shift_right_logical(code, 6), 63)


def item_shifts(code):
    shift_a = lax.bitwise_and(lax.shift_right_logical(code, 12), 3) - 1
    shift_b = lax.shift_right_logical(code, 14) - 1
    return shift_a.astype(jnp.float32) * UNIT, shift_b.astype(jnp.float32) * UNIT


def list_items(items_ref, candidates, pair_ref):
    cols = pair_ref.shape[1]
    count = jnp.int32(0)
    for k, own, code in candidates:
        items_ref[count + 1] = code
        count = count + jnp.where(pair_ref[own // cols, own % cols, k] > 0, 1, 0)
    items_ref[0] = count
    items_ref[count + 1] = NO_ITEM


def inner_candidates(rows, cols):
    found = []
    for k in range(4):
        shift_a, shift_b = OFFSETS[k]
        for a in range(rows):
            for b in range(cols):
                if 0 <= a + shift_a < rows and 0 <= b + shift_b < cols:
                    own = a * cols + b
                    other = own + shift_a * cols + shift_b
                    found.append((k, own, item_code(own, other, shift_a, shift_b)))
    return found


def cross_candidates(rows, cols):
    places = [(-1, b) for b in range(cols)] + [(rows, b) for b in range(cols)]
    places += [(a, -1) for a in range(-1, rows + 1)] + [(a, cols) for a in range(-1, rows + 1)]
    found = []
    for k in range(8):
        shift_a, shift_b = OFFSETS[k]
        for a in range(rows):
            for b in range(cols):
                place = (a + shift_a, b + shift_b)
                if place in places:
                    own = a * cols + b
                    found.append((k, own, item_code(own, places.index(place), -shift_a, -shift_b)))
    return found


def pack_kernel(v_hbm, c_hbm, pair_hbm, first_ref, last_ref, edge_ref, v_ref, c_ref, pair_ref, sems):
    rows, cols, rhs = v_hbm.shape[:3]
    fetches = []
    for row in range(rows):
        own = pl.ds(row * cols, cols)
        fetches.append(pltpu.make_async_copy(v_hbm.at[row], v_ref.at[own], sems.at[2 * row]))
        fetches.append(pltpu.make_async_copy(c_hbm.at[row], c_ref.at[own], sems.at[2 * row + 1]))
    fetches.append(pltpu.make_async_copy(pair_hbm, pair_ref, sems.at[2 * rows]))
    for fetch in fetches:
        fetch.start()
    for fetch in fetches:
        fetch.wait()
    both = slice(rhs, rhs + 2)
    for row in range(rows):
        for column_ref, at in ((first_ref, row * cols), (last_ref, row * cols + cols - 1)):
            column_ref[row, 0:rhs] = v_ref[at]
            column_ref[row, both] = c_ref[at]
    for n, row in enumerate((0, rows - 1)):
        own = slice(row * cols, (row + 1) * cols)
        edge_ref[n, :, 0:rhs] = v_ref[own]
        edge_ref[n, :, both] = c_ref[own]


def use_own(out_ref, parts_ref, high, low, at):
    out_ref[at] += product(dot_nn, parts_ref, at, high, low)


def use_pair(out_ref, parts_ref, items_ref, high, low, n):
    own, other = item_blocks(items_ref[n + 1])
    out_ref[own] += product(dot_nn, parts_ref, other, high, low)
    out_ref[other] += product(dot_nt, parts_ref, own, high, low)


def use_cross(out_ref, parts_ref, items_ref, high, low, n):
    own, other = item_blocks(items_ref[n + 1])
    out_ref[own] += product(dot_nt, parts_ref, other, high, low)


def own_first_kernel(
    pair_ref, v_ref, c_ref, near_ref, cross_ref, out_ref, kept_ref, parts_ref, points_ref, spread_ref
):
    rows, cols = pair_ref.shape[:2]
    lanes = spread_ref.shape[3]

    def one(at):
        store_parts(parts_ref, at, v_ref[at])
        out_ref[at] = NUGGET * v_ref[at]
        scaled = c_ref[at] * UNIT
        points_ref[at] = scaled
        for axis in range(2):
            spread_ref[at, axis] = across_lanes(scaled[axis : axis + 1], lanes)
        make_tile(kept_ref, at, spread_ref, at, points_ref, at, 0.0, 0.0)

    def one_pair(turn, carry):
        one(2 * turn)
        one(2 * turn + 1)
        return carry

    lax.fori_loop(0, rows * cols // 2, one_pair, 0)
    only_use(0, jnp.int32(rows * cols), kept_ref, functools.partial(use_own, out_ref, parts_ref))
    list_items(near_ref, inner_candidates(rows, cols), pair_ref)
    list_items(cross_ref, cross_candidates(rows, cols), pair_ref)


def inner_first_kernel(items_ref, sum_ref, parts_ref, points_ref, spread_ref, out_ref, kept_ref):
    out_ref[...] = sum_ref[...]

    def make(n):
        code = items_ref[n + 1]
        own, other = item_blocks(code)
        make_tile(kept_ref, n, spread_ref, other, points_ref, own, *item_shifts(code))

    in_turns(items_ref[0], make)
    only_use(0, items_ref[0], kept_ref, functools.partial(use_pair, out_ref, parts_ref, items_ref))


def take_round(round_refs, rhs, parts_ref, points_ref=None):
    start = 0
    for side in round_refs:

        def take(at, carry, side=side, start=start):
            store_parts(parts_ref, start + at, side[at, 0:rhs])
            if points_ref is not None:
                points_ref[start + at] = side[at, rhs : rhs + 2] * UNIT
            return carry

        lax.fori_loop(0, side.shape[0], take, 0)
        start += side.shape[0]


def cross_first_kernel(
    items_ref, sum_ref, north_ref, south_ref, west_ref, east_ref, spread_ref,
    out_ref, kept_ref, parts_ref, points_ref
):
    out_ref[...] = sum_ref[...]
    take_round((north_ref, south_ref, west_ref, east_ref), sum_ref.shape[1], parts_ref, points_ref)

    def make(n):
        code = items_ref[n + 1]
        own, other = item_blocks(code)
        make_tile(kept_ref, n, spread_ref, own, points_ref, other, *item_shifts(code))

    in_turns(items_ref[0], make)
    only_use(0, items_ref[0], kept_ref, functools.partial(use_cross, out_ref, parts_ref, items_ref))


def first_share(count):
    return lax.shift_right_logical(5 * count, 3)


def near_again_kernel(items_ref, v_ref, own_ref, kept_ref, out_ref, parts_ref):
    def one(at, carry):
        store_parts(parts_ref, at, v_ref[at])
        out_ref[at] = NUGGET * v_ref[at]
        return carry

    lax.fori_loop(0, parts_ref.shape[0], one, 0, unroll=2)
    only_use(0, jnp.int32(parts_ref.shape[0]), own_ref, functools.partial(use_own, out_ref, parts_ref))
    use = functools.partial(use_pair, out_ref, parts_ref, items_ref)
    only_use(0, first_share(items_ref[0]), kept_ref, use)


def rest_again_kernel(items_ref, sum_ref, parts_ref, kept_ref, out_ref):
    out_ref[...] = sum_ref[...]
    use = functools.partial(use_pair, out_ref, parts_ref, items_ref)
    only_use(first_share(items_ref[0]), items_ref[0], kept_ref, use)


def cross_again_kernel(
    items_ref, sum_ref, north_ref, south_ref, west_ref, east_ref, kept_ref, v0_ref, v1_ref,
    out_ref, moments_ref, parts_ref
):
    out_ref[...] = sum_ref[...]
    take_round((north_ref, south_ref, west_ref, east_ref), sum_ref.shape[1], parts_ref)
    only_use(0, items_ref[0], kept_ref, functools.partial(use_cross, out_ref, parts_ref, items_ref))
    zero = jnp.zeros(out_ref.shape[1:], jnp.float32)

    def gather(at, sums):
        w0, w1, w2 = v0_ref[at], v1_ref[at], out_ref[at]
        terms = (w0 * w0, w0 * w1, w1 * w1, w1 * w2)
        return tuple(s + t for s, t in zip(sums, terms))

    sums = lax.fori_loop(0, out_ref.shape[0], gather, (zero,) * 4)
    lanes = moments_ref.shape[2]
    folded = [sum(s[:, left : left + lanes] for left in range(0, s.shape[1], lanes)) for s in sums]
    stacked = jnp.concatenate(folded, axis=0)
    line = jnp.sum(jnp.transpose(stacked), axis=0, keepdims=True)
    moments_ref[...] = jnp.broadcast_to(line[None], moments_ref.shape)


def final_kernel(moments_ref, v0_ref, v1_ref, v2_ref, solution_ref, residual_ref):
    rhs, points = v0_ref.shape[1:]
    line = moments_ref[0]
    for at in range(1, moments_ref.shape[0]):
        line = line + moments_ref[at]
    table = across_lanes(line, line.shape[1])
    m00, m01, m11, m12 = (table[k * rhs : (k + 1) * rhs] for k in range(4))
    a = m00 / m01
    norm = m00 - 2.0 * a * m01 + a * a * m11
    grow = 1.0 + norm / m00
    step = norm / (grow * (grow * m01 - 2.0 * a * m11) + a * a * m12)
    first = jnp.concatenate([a + step * grow] * (points // line.shape[1]), axis=1)
    second = jnp.concatenate([step * a] * (points // line.shape[1]), axis=1)

    def one(at, carry):
        w0, w1, w2 = v0_ref[at], v1_ref[at], v2_ref[at]
        solution_ref[at] = first * w0 - second * w1
        residual_ref[at] = w0 - first * w1 + second * w2
        return carry

    lax.fori_loop(0, v0_ref.shape[0], one, 0)


def swapped(first, last, axis):
    count = lax.axis_size(axis)
    even = lax.rem(lax.axis_index(axis), 2) == 0
    swap_up = [(i, i ^ 1) for i in range(count) if i ^ 1 < count]
    swap_down = [(i, ((i + 1) ^ 1) - 1) for i in range(count) if 0 <= ((i + 1) ^ 1) - 1 < count]
    got_up = lax.ppermute(jnp.where(even, last, first), axis, swap_up)
    got_down = lax.ppermute(jnp.where(even, first, last), axis, swap_down)
    return jnp.where(even, got_down, got_up), jnp.where(even, got_up, got_down)


def on_device(kernel, outputs, inputs, scratch=(), listed=False, products=0, made=0, where=pltpu.VMEM):
    vmem = pl.BlockSpec(memory_space=pltpu.VMEM)
    smem = pl.BlockSpec(memory_space=pltpu.SMEM)
    source = pl.BlockSpec(memory_space=where)
    return pl.pallas_call(
        kernel,
        out_shape=tuple(outputs),
        in_specs=[smem if listed and n == 0 else source for n in range(len(inputs))],
        out_specs=tuple(smem if out.dtype == jnp.int32 else vmem for out in outputs),
        scratch_shapes=list(scratch),
        compiler_params=pltpu.CompilerParams(vmem_limit_bytes=VMEM_LIMIT),
        cost_estimate=pl.CostEstimate(
            flops=products, transcendentals=made, bytes_accessed=sum(4 * x.size for x in inputs)
        ),
        name=kernel.__name__,
    )(*inputs)


def tiles(count, points):
    return jax.ShapeDtypeStruct((count, 2, points, points), jnp.bfloat16)


def per_device(right_side, coords, pair_list):
    pair_list = jnp.transpose(pair_list, (1, 2, 0))
    rows, cols, rhs, points = right_side.shape
    blocks = rows * cols
    devices = lax.axis_size("region") * lax.axis_size("tile")
    lanes = 128
    f32, bf16, i32 = jnp.float32, jnp.bfloat16, jnp.int32
    array = jax.ShapeDtypeStruct
    halo = 2 * rows + 2 * (cols + 2)
    near_count = len(inner_candidates(rows, cols))
    cross_count = len(cross_candidates(rows, cols))
    field = array((blocks, rhs, points), f32)
    column = array((rows, rhs + 2, points), f32)
    parts_round = pltpu.VMEM((halo, 2 * rhs, points), bf16)
    each = 6 * rhs * points * points

    def columns_round(first, last, north, south):
        first = jnp.concatenate([north[:1], first, south[:1]], axis=0)
        last = jnp.concatenate([north[cols - 1 :], last, south[cols - 1 :]], axis=0)
        return swapped(first, last, "tile")

    fetched = (
        column, column, array((2, cols, rhs + 2, points), f32), field, array((blocks, 2, points), f32),
        array(pair_list.shape, i32),
    )
    first, last, edges, w0, stations, pairs = on_device(
        pack_kernel, fetched,
        tuple(pltpu.with_memory_space_constraint(x, pltpu.HBM) for x in (right_side, coords, pair_list)),
        (pltpu.SemaphoreType.DMA((2 * rows + 1,)),), where=pltpu.HBM,
    )
    north, south = swapped(edges[0], edges[1], "region")
    parts_field = array((blocks, 2 * rhs, points), bf16)
    near_items, cross_items, part, own_tiles, parts, own_points, spread = on_device(
        own_first_kernel,
        (array((near_count + 3,), i32), array((cross_count + 3,), i32), field, tiles(blocks, points), parts_field,
         array((blocks, 2, points), f32), array((blocks, 2, points, lanes), f32)),
        (pairs, w0, stations), listed=True, products=blocks * each, made=blocks * 2 * points * points,
    )
    north, south, part = lax.optimization_barrier((north, south, part))
    west, east = columns_round(first, last, north, south)
    part, near_tiles = on_device(
        inner_first_kernel, (field, tiles(near_count + 2, points)), (near_items, part, parts, own_points, spread),
        (), True, near_count * each, near_count * 2 * points * points,
    )
    w1, cross_tiles = on_device(
        cross_first_kernel, (field, tiles(cross_count + 2, points)),
        (cross_items, part, north, south, west, east, spread),
        (parts_round, pltpu.VMEM((halo, 2, points), f32)), True,
        cross_count * each, cross_count * 2 * points * points,
    )
    w1_grid = w1.reshape(right_side.shape)
    north, south = swapped(w1_grid[0], w1_grid[rows - 1], "region")
    part, parts = on_device(
        near_again_kernel, (field, parts_field), (near_items, w1, own_tiles, near_tiles), (), True,
        (blocks + near_count) * each,
    )
    north, south, part = lax.optimization_barrier((north, south, part))
    west, east = columns_round(w1_grid[:, 0], w1_grid[:, cols - 1], north, south)
    (part,) = on_device(
        rest_again_kernel, (field,), (near_items, part, parts, near_tiles), (), True, near_count * each
    )
    w2, moments = on_device(
        cross_again_kernel, (field, array((devices, 1, 4 * rhs), f32)),
        (cross_items, part, north, south, west, east, cross_tiles, w0, w1), (parts_round,), True, cross_count * each,
    )
    moments = lax.all_to_all(moments, ("region", "tile"), 0, 0)
    solution, residual = on_device(final_kernel, (field, field), (moments, w0, w1, w2))
    return solution.reshape(right_side.shape), residual.reshape(right_side.shape)


def solution(mesh):
    placed = (
        P("region", "tile", None, None),
        P("region", "tile", None, None),
        P(None, "region", "tile"),
    )
    return jax.shard_map(
        per_device,
        mesh=mesh,
        in_specs=placed,
        out_specs=(P("region", "tile", None, None), P("region", "tile", None, None)),
        check_vma=False,
    )
```

profile of v0, /device:TPU:0, one launch (start us, length us, event | category | flops | bytes accessed | tf_op | source)
XLA Modules:
  0.0 73.4 jit_solution(15353532931758685253)
XLA Ops:
  0.6 2.0 %pack_kernel.1 = (f32[4,34,256]{2,1,0:T(8,128)S(1)}, f32[4,34,256]{2,1,0:T(8,128)S(1)}, f32[2,4,34,256]{3,2,1,0:T(8,128)S(1)}, f32[16,32,256]{2,1,0:T(8,128)S(1)...) custom-call(f32[4,4,32,256]{3,2,1,0:T(8,128)} %v_hbm.1, f32[4,4,2,256]{3,2,1,0:T(2,128)} %c_hbm.1, s32[4,4,8]{2,1,0:T(4,128)} %bitcast.17), custom_call_target="tpu_custom_call" | custom-call | bytes 557568 | tf_op jit(solution)/shard_map/pack_kernel/pallas_call | solution.py:336
  2.7 3.0 %collective-permute-start.1 = (f32[4,34,256]{2,1,0:T(8,128)S(1)}, f32[4,34,256]{2,1,0:T(8,128)S(1)}, u32[]{:S(2)}, u32[]{:S(2)}) collective-permute-start(f32[4,34,256]{2,1,0:T(8,128)S(1)} %get-tuple-element.74), channel_id=1, source_target_pairs={{0,8},{8,0},{16,24},{24,16},{1,9},{9,1},{17,25},{25,17},{2,10},{10... | collective-permute-start | bytes 417800 | tf_op jit(solution)/shard_map/ppermute | solution.py:327
  5.7 0.7 collective-permute-start
  6.4 6.0 %own_first_kernel.1 = (s32[45]{0:T(128)S(1)}, s32[47]{0:T(128)S(1)}, f32[16,32,256]{2,1,0:T(8,128)S(1)}, bf16[16,2,256,256]{3,2,1,0:T(8,128)(2,1)S(1)}, bf16[16,...) custom-call(s32[4,4,8]{2,1,0:T(4,128)S(1)} %get-tuple-element.31.pair_ref, ...), custom_call_target="tpu_custom_call" | custom-call | flops 201326592 | bytes 557568 | tf_op jit(solution)/shard_map/own_first_kernel/pallas_call | solution.py:336
  12.4 0.0 collective-permute-done.1
  12.4 0.0 collective-permute-done
  12.5 0.1 collective-permute-start.3
  12.6 0.7 collective-permute-start.2
  13.2 3.3 %inner_first_kernel.1 = (f32[16,32,256]{2,1,0:T(8,128)S(1)}, bf16[44,2,256,256]{3,2,1,0:T(8,128)(2,1)S(1)}) custom-call(s32[45]{0:T(128)S(1)} %get-tuple-element.35.items_ref, f32[16,32,256]{2,1,0:T(8,128)S(1)} %get-tuple-element.38.sum_ref, bf16[16,64,256]{2,1,0:T(8,128)(2,1)S(1)} %get-tuple-element.39.parts_ref, ...), custom_call_target="tpu_custom_call" | custom-call | flops 528482304 | bytes 5800116 | tf_op jit(solution)/shard_map/inner_first_kernel/pallas_call | solution.py:336
  16.5 0.0 collective-permute-done.3
  16.5 0.0 collective-permute-done.2
  16.6 2.1 %cross_first_kernel.1 = (f32[16,32,256]{2,1,0:T(8,128)S(1)}, bf16[46,2,256,256]{3,2,1,0:T(8,128)(2,1)S(1)}) custom-call(s32[47]{0:T(128)S(1)} %get-tuple-element.34.items_ref, f32[16,32,256]{2,1,0:T(8,128)S(1)} %get-tuple-element.42.sum_ref, f32[4,34,256]{2,1,0:T(8,128)S(1)} %get-tuple-element.43.north_ref, f32[4,34,256]{2,1,0:T(8,128)S(1)} %get-tuple-element.44.south_ref, ...), custom_call_target="tpu_custom_call" | custom-call | flops 553648128 | bytes 5415100 | tf_op jit(solution)/shard_map/cross_first_kernel/pallas_call | solution.py:336
  18.8 5.7 %collective-permute-start.5 = (f32[4,32,256]{2,1,0:T(8,128)S(1)}, f32[4,32,256]{2,1,0:T(8,128)S(1)}, u32[]{:S(2)}, u32[]{:S(2)}) collective-permute-start(f32[4,32,256]{2,1,0:T(8,128)S(1)} %get-tuple-element.62), channel_id=1, source_target_pairs={{0,8},{8,0},{16,24},{24,16},{1,9},{9,1},{17,25},{25,17},{2,10},{10... | collective-permute-start | bytes 393224 | tf_op jit(solution)/shard_map/ppermute | solution.py:327
  24.5 0.7 collective-permute-start.4
  25.1 2.4 %near_again_kernel.1 = (f32[16,32,256]{2,1,0:T(8,128)S(1)}, bf16[16,64,256]{2,1,0:T(8,128)(2,1)S(1)}) custom-call(s32[45]{0:T(128)S(1)} %get-tuple-element.35.items_ref, f32[16,32,256]{2,1,0:T(8,128)S(1)} %get-tuple-element.47.v_ref.v1_ref, bf16[16,2,256,256]{3,2,1,0:T(8,128)(2,1)S(1)} %get-tuple-element.48.own_ref, ...), custom_call_target="tpu_custom_call" | custom-call | flops 729808896 | bytes 31981748 | tf_op jit(solution)/shard_map/near_again_kernel/pallas_call | solution.py:336
  27.5 0.0 collective-permute-done.5
  27.5 0.0 collective-permute-done.4
  27.6 5.2 %collective-permute-start.7 = (f32[6,32,256]{2,1,0:T(8,128)S(1)}, f32[6,32,256]{2,1,0:T(8,128)S(1)}, u32[]{:S(2)}, u32[]{:S(2)}) collective-permute-start(f32[6,32,256]{2,1,0:T(8,128)S(1)} %get-tuple-element.70), channel_id=1, source_target_pairs={{0,1},{1,0},{2,3},{3,2},{4,5},{5,4},{6,7},{7,6},{8,9},{9,8},{10,11... | collective-permute-start | bytes 589832 | tf_op jit(solution)/shard_map/ppermute | solution.py:327
  32.8 0.7 collective-permute-start.6
  33.5 1.4 %rest_again_kernel.1.sum_ref = f32[16,32,256]{2,1,0:T(8,128)S(1)} custom-call(s32[45]{0:T(128)S(1)} %get-tuple-element.35.items_ref, f32[16,32,256]{2,1,0:T(8,128)S(1)} %get-tuple-element.51.sum_ref, bf16[16,64,256]{2,1,0:T(8,128)(2,1)S(1)} %get-tuple-element.52.parts_ref, bf16[44,2,256,256]{3,2,1,0:T(8,128)(2,1)S(1)} %get-tuple-element.49.kept_ref), custom_call_target="tpu_custom_call" | custom-call | flops 528482304 | bytes 24641716 | tf_op jit(solution)/shard_map/rest_again_kernel/pallas_call | solution.py:336
  34.9 0.0 collective-permute-done.7
  34.9 0.0 collective-permute-done.6
  34.9 1.8 %cross_again_kernel.1 = (f32[16,32,256]{2,1,0:T(8,128)S(1)}, f32[32,1,128]{2,1,0:T(1,128)S(1)}) custom-call(s32[47]{0:T(128)S(1)} %get-tuple-element.34.items_ref, f32[16,32,256]{2,1,0:T(8,128)S(1)} %rest_again_kernel.1.sum_ref, f32[4,32,256]{2,1,0:T(8,128)S(1)} %get-tuple-element.53.north_ref, f32[4,32,256]{2,1,0:T(8,128)S(1)} %get-tuple-element.54.south_ref, ...), custom_call_target="tpu_custom_call" | custom-call | flops 553648128 | bytes 26345660 | tf_op jit(solution)/shard_map/cross_again_kernel/pallas_call | solution.py:336
  36.8 35.3 %all_to_all.5.moments_ref = f32[32,1,128]{2,1,0:T(1,128)S(1)} all-to-all(f32[32,1,128]{2,1,0:T(1,128)S(1)} %get-tuple-element.56), channel_id=1, replica_groups=mesh['region'=4,'tile'=8] {'region','tile'}, dimensions={0} | all-to-all | bytes 32768 | tf_op jit(solution)/shard_map/all_to_all | solution.py:419
  72.1 1.3 %final_kernel.1 = (f32[16,32,256]{2,1,0:T(8,128)}, f32[16,32,256]{2,1,0:T(8,128)}) custom-call(f32[32,1,128]{2,1,0:T(1,128)S(1)} %all_to_all.5.moments_ref, f32[16,32,256]{2,1,0:T(8,128)S(1)} %get-tuple-element.32.v_ref.v0_ref, f32[16,32,256]{2,1,0:T(8,128)S(1)} %get-tuple-element.47.v_ref.v1_ref, f32[16,32,256]{2,1,0:T(8,128)S(1)} %get-tuple-element.57.v2_ref), custom_call_target="tpu_custom_call" | custom-call | bytes 1589248 | tf_op jit(solution)/shard_map/final_kernel/pallas_call | solution.py:336
  (12 shorter events, 0.3 us)
Async XLA Ops:
  2.7 9.7 %collective-permute-start.1 = (f32[4,34,256]{2,1,0:T(8,128)S(1)}, f32[4,34,256]{2,1,0:T(8,128)S(1)}, u32[]{:S(2)}, u32[]{:S(2)}) collective-permute-start(f32[4,34,256]{2,1,0:T(8,128)S(1)} %get-tuple-element.74), channel_id=1, source_target_pairs={{0,8},{8,0},{16,24},{24,16},{1,9},{9,1},{17,25},{25,17},{2,10},{10... | collective-permute-start | bytes 417800 | tf_op jit(solution)/shard_map/ppermute | solution.py:327
  5.7 6.7 %collective-permute-start = (f32[4,34,256]{2,1,0:T(8,128)S(1)}, f32[4,34,256]{2,1,0:T(8,128)S(1)}, u32[]{:S(2)}, u32[]{:S(2)}) collective-permute-start(f32[4,34,256]{2,1,0:T(8,128)S(1)} %get-tuple-element.75), channel_id=1, source_target_pairs={{8,16},{16,8},{9,17},{17,9},{10,18},{18,10},{11,19},{19,11},{12,20... | collective-permute-start | bytes 417800 | tf_op jit(solution)/shard_map/ppermute | solution.py:328
  12.5 4.1 %collective-permute-start.3 = (f32[6,34,256]{2,1,0:T(8,128)S(1)}, f32[6,34,256]{2,1,0:T(8,128)S(1)}, u32[]{:S(2)}, u32[]{:S(2)}) collective-permute-start(f32[6,34,256]{2,1,0:T(8,128)S(1)} %get-tuple-element.66), channel_id=1, source_target_pairs={{0,1},{1,0},{2,3},{3,2},{4,5},{5,4},{6,7},{7,6},{8,9},{9,8},{10,11... | collective-permute-start | bytes 626696 | tf_op jit(solution)/shard_map/ppermute | solution.py:327
  12.6 4.0 %collective-permute-start.2 = (f32[6,34,256]{2,1,0:T(8,128)S(1)}, f32[6,34,256]{2,1,0:T(8,128)S(1)}, u32[]{:S(2)}, u32[]{:S(2)}) collective-permute-start(f32[6,34,256]{2,1,0:T(8,128)S(1)} %get-tuple-element.67), channel_id=1, source_target_pairs={{1,2},{2,1},{3,4},{4,3},{5,6},{6,5},{9,10},{10,9},{11,12},{12,11},... | collective-permute-start | bytes 626696 | tf_op jit(solution)/shard_map/ppermute | solution.py:328
  18.8 8.8 %collective-permute-start.5 = (f32[4,32,256]{2,1,0:T(8,128)S(1)}, f32[4,32,256]{2,1,0:T(8,128)S(1)}, u32[]{:S(2)}, u32[]{:S(2)}) collective-permute-start(f32[4,32,256]{2,1,0:T(8,128)S(1)} %get-tuple-element.62), channel_id=1, source_target_pairs={{0,8},{8,0},{16,24},{24,16},{1,9},{9,1},{17,25},{25,17},{2,10},{10... | collective-permute-start | bytes 393224 | tf_op jit(solution)/shard_map/ppermute | solution.py:327
  24.5 3.1 %collective-permute-start.4 = (f32[4,32,256]{2,1,0:T(8,128)S(1)}, f32[4,32,256]{2,1,0:T(8,128)S(1)}, u32[]{:S(2)}, u32[]{:S(2)}) collective-permute-start(f32[4,32,256]{2,1,0:T(8,128)S(1)} %get-tuple-element.63), channel_id=1, source_target_pairs={{8,16},{16,8},{9,17},{17,9},{10,18},{18,10},{11,19},{19,11},{12,20... | collective-permute-start | bytes 393224 | tf_op jit(solution)/shard_map/ppermute | solution.py:328
  27.6 7.2 %collective-permute-start.7 = (f32[6,32,256]{2,1,0:T(8,128)S(1)}, f32[6,32,256]{2,1,0:T(8,128)S(1)}, u32[]{:S(2)}, u32[]{:S(2)}) collective-permute-start(f32[6,32,256]{2,1,0:T(8,128)S(1)} %get-tuple-element.70), channel_id=1, source_target_pairs={{0,1},{1,0},{2,3},{3,2},{4,5},{5,4},{6,7},{7,6},{8,9},{9,8},{10,11... | collective-permute-start | bytes 589832 | tf_op jit(solution)/shard_map/ppermute | solution.py:327
  32.8 2.1 %collective-permute-start.6 = (f32[6,32,256]{2,1,0:T(8,128)S(1)}, f32[6,32,256]{2,1,0:T(8,128)S(1)}, u32[]{:S(2)}, u32[]{:S(2)}) collective-permute-start(f32[6,32,256]{2,1,0:T(8,128)S(1)} %get-tuple-element.71), channel_id=1, source_target_pairs={{1,2},{2,1},{3,4},{4,3},{5,6},{6,5},{9,10},{10,9},{11,12},{12,11},... | collective-permute-start | bytes 589832 | tf_op jit(solution)/shard_map/ppermute | solution.py:328
where the time goes:
time: 72.6 us; the launch traced here: 73.4 us
  blocking collectives  35.3 us (49%)
  Pallas kernels  20.3 us (28%)
  starting transfers between devices  16.6 us (23%)
  between operations  0.88 us (1%)
    all_to_all x1, blocking collectives, per_device(): moments = lax.all_to_all(moments, ('region', 'tile'), 0, 0)  35.3 us
    pallas_call x8, Pallas kernels, on_device(): pl.pallas_call(kernel, out_shape=tuple(outputs), in_specs=[smem if listed...  20.3 us
    ppermute x4, starting transfers between devices, swapped(): got_up = lax.ppermute(jnp.where(even, last, first), axis, swap_up)  14 us
    ppermute x4, starting transfers between devices, swapped(): got_down = lax.ppermute(jnp.where(even, first, last), axis, swap_down)  2.65 us
  transfers between devices with their start and end apart: 8, of which 0 were waited for; matrix products, arithmetic and copies ran while one was open for 0% of the time, Pallas kernels for 18%

commit v1 on v0

--- a/solution.py
+++ b/solution.py
@@ -98,6 +98,10 @@
 NO_ITEM = item_code(0, 0, 2, 2)
 
 
+def item_blocks_of(code):
+    return code % 64, code // 64 % 64
+
+
 def item_blocks(code):
     return lax.bitwise_and(code, 63), lax.bitwise_and(lax.shift_right_logical(code, 6), 63)
 
@@ -108,12 +112,15 @@
     return shift_a.astype(jnp.float32) * UNIT, shift_b.astype(jnp.float32) * UNIT
 
 
-def list_items(items_ref, candidates, pair_ref):
+def list_items(items_ref, candidates, pair_ref, more=()):
     cols = pair_ref.shape[1]
     count = jnp.int32(0)
-    for k, own, code in candidates:
-        items_ref[count + 1] = code
-        count = count + jnp.where(pair_ref[own // cols, own % cols, k] > 0, 1, 0)
+    for part in (candidates, more):
+        for k, own, code in part:
+            items_ref[count + 1] = code
+            count = count + jnp.where(pair_ref[own // cols, own % cols, k] > 0, 1, 0)
+        if part is candidates:
+            items_ref[len(candidates) + len(more) + 2] = count
     items_ref[0] = count
     items_ref[count + 1] = NO_ITEM
 
@@ -143,7 +150,8 @@
                 if place in places:
                     own = a * cols + b
                     found.append((k, own, item_code(own, places.index(place), -shift_a, -shift_b)))
-    return found
+    in_rows = [item for item in found if item_blocks_of(item[2])[1] < 2 * cols]
+    return in_rows, [item for item in found if item not in in_rows]
 
 
 def pack_kernel(v_hbm, c_hbm, pair_hbm, first_ref, last_ref, edge_ref, v_ref, c_ref, pair_ref, sems):
@@ -207,7 +215,8 @@
     lax.fori_loop(0, rows * cols // 2, one_pair, 0)
     only_use(0, jnp.int32(rows * cols), kept_ref, functools.partial(use_own, out_ref, parts_ref))
     list_items(near_ref, inner_candidates(rows, cols), pair_ref)
-    list_items(cross_ref, cross_candidates(rows, cols), pair_ref)
+    in_rows, in_columns = cross_candidates(rows, cols)
+    list_items(cross_ref, in_rows, pair_ref, in_columns)
 
 
 def inner_first_kernel(items_ref, sum_ref, parts_ref, points_ref, spread_ref, out_ref, kept_ref):
@@ -222,8 +231,7 @@
     only_use(0, items_ref[0], kept_ref, functools.partial(use_pair, out_ref, parts_ref, items_ref))
 
 
-def take_round(round_refs, rhs, parts_ref, points_ref=None):
-    start = 0
+def take_round(round_refs, rhs, parts_ref, points_ref=None, start=0):
     for side in round_refs:
 
         def take(at, carry, side=side, start=start):
@@ -268,19 +276,25 @@
     only_use(0, first_share(items_ref[0]), kept_ref, use)
 
 
-def rest_again_kernel(items_ref, sum_ref, parts_ref, kept_ref, out_ref):
-    out_ref[...] = sum_ref[...]
-    use = functools.partial(use_pair, out_ref, parts_ref, items_ref)
-    only_use(first_share(items_ref[0]), items_ref[0], kept_ref, use)
-
-
-def cross_again_kernel(
-    items_ref, sum_ref, north_ref, south_ref, west_ref, east_ref, kept_ref, v0_ref, v1_ref,
-    out_ref, moments_ref, parts_ref
+def rest_again_kernel(
+    near_ref, cross_ref, sum_ref, parts_ref, near_kept_ref, north_ref, south_ref, cross_kept_ref, out_ref, round_ref
 ):
     out_ref[...] = sum_ref[...]
-    take_round((north_ref, south_ref, west_ref, east_ref), sum_ref.shape[1], parts_ref)
-    only_use(0, items_ref[0], kept_ref, functools.partial(use_cross, out_ref, parts_ref, items_ref))
+    use = functools.partial(use_pair, out_ref, parts_ref, near_ref)
+    only_use(first_share(near_ref[0]), near_ref[0], near_kept_ref, use)
+    take_round((north_ref, south_ref), sum_ref.shape[1], round_ref)
+    in_rows = cross_ref[cross_ref.shape[0] - 1]
+    only_use(0, in_rows, cross_kept_ref, functools.partial(use_cross, out_ref, round_ref, cross_ref))
+
+
+def cross_again_kernel(
+    items_ref, sum_ref, west_ref, east_ref, kept_ref, v0_ref, v1_ref, out_ref, moments_ref, parts_ref
+):
+    out_ref[...] = sum_ref[...]
+    start = parts_ref.shape[0] - west_ref.shape[0] - east_ref.shape[0]
+    take_round((west_ref, east_ref), sum_ref.shape[1], parts_ref, start=start)
+    in_rows = items_ref[items_ref.shape[0] - 1]
+    only_use(in_rows, items_ref[0], kept_ref, functools.partial(use_cross, out_ref, parts_ref, items_ref))
     zero = jnp.zeros(out_ref.shape[1:], jnp.float32)
 
     def gather(at, sums):
@@ -336,7 +350,7 @@
     return pl.pallas_call(
         kernel,
         out_shape=tuple(outputs),
-        in_specs=[smem if listed and n == 0 else source for n in range(len(inputs))],
+        in_specs=[smem if listed and x.dtype == jnp.int32 else source for x in inputs],
         out_specs=tuple(smem if out.dtype == jnp.int32 else vmem for out in outputs),
         scratch_shapes=list(scratch),
         compiler_params=pltpu.CompilerParams(vmem_limit_bytes=VMEM_LIMIT),
@@ -361,7 +375,7 @@
     array = jax.ShapeDtypeStruct
     halo = 2 * rows + 2 * (cols + 2)
     near_count = len(inner_candidates(rows, cols))
-    cross_count = len(cross_candidates(rows, cols))
+    cross_count = sum(len(part) for part in cross_candidates(rows, cols))
     field = array((blocks, rhs, points), f32)
     column = array((rows, rhs + 2, points), f32)
     parts_round = pltpu.VMEM((halo, 2 * rhs, points), bf16)
@@ -410,11 +424,13 @@
     north, south, part = lax.optimization_barrier((north, south, part))
     west, east = columns_round(w1_grid[:, 0], w1_grid[:, cols - 1], north, south)
     (part,) = on_device(
-        rest_again_kernel, (field,), (near_items, part, parts, near_tiles), (), True, near_count * each
+        rest_again_kernel, (field,),
+        (near_items, cross_items, part, parts, near_tiles, north, south, cross_tiles), (parts_round,), True,
+        near_count * each,
     )
     w2, moments = on_device(
         cross_again_kernel, (field, array((devices, 1, 4 * rhs), f32)),
-        (cross_items, part, north, south, west, east, cross_tiles, w0, w1), (parts_round,), True, cross_count * each,
+        (cross_items, part, west, east, cross_tiles, w0, w1), (parts_round,), True, cross_count * each,
     )
     moments = lax.all_to_all(moments, ("region", "tile"), 0, 0)
     solution, residual = on_device(final_kernel, (field, field), (moments, w0, w1, w2))

time: 72.6 us -> 72.4 us (level); the launches traced: 73.4 us -> 71.4 us
  blocking collectives: 35.3 us -> 21.4 us
  starting transfers between devices: 16.6 us -> 28.1 us
    all_to_all x1, blocking collectives: 35.3 us -> 21.4 us  [per_device(): moments = lax.all_to_all(moments, ('region', 'tile'), 0, 0)]
    ppermute x4, starting transfers between devices: 14 us -> 25.4 us  [swapped(): got_up = lax.ppermute(jnp.where(even, last, first), axis, swap_up)]
  transfers between devices with their start and end apart: 8 -> 8, of which waited for: 0 -> 0; matrix products, arithmetic and copies ran while one was open for 0% -> 0% of each run, Pallas kernels for 18% -> 19%
where the time goes in v1:
time: 72.4 us; the launch traced here: 71.4 us
  starting transfers between devices  28.1 us (39%)
  blocking collectives  21.4 us (30%)
  Pallas kernels  20.7 us (29%)
  between operations  0.89 us (1%)
    ppermute x4, starting transfers between devices, swapped(): got_up = lax.ppermute(jnp.where(even, last, first), axis, swap_up)  25.4 us
    all_to_all x1, blocking collectives, per_device(): moments = lax.all_to_all(moments, ('region', 'tile'), 0, 0)  21.4 us
    pallas_call x8, Pallas kernels, on_device(): pl.pallas_call(kernel, out_shape=tuple(outputs), in_specs=[smem if listed...  20.7 us
    ppermute x4, starting transfers between devices, swapped(): got_down = lax.ppermute(jnp.where(even, first, last), axis, swap_down)  2.65 us
  transfers between devices with their start and end apart: 8, of which 0 were waited for; matrix products, arithmetic and copies ran while one was open for 0% of the time, Pallas kernels for 19%

profile of v1, /device:TPU:0, one launch (start us, length us, event | category | flops | bytes accessed | tf_op | source)
XLA Modules:
  0.0 71.4 jit_solution(11477784391534351728)
XLA Ops:
  0.6 2.0 %pack_kernel.1 = (f32[4,34,256]{2,1,0:T(8,128)S(1)}, f32[4,34,256]{2,1,0:T(8,128)S(1)}, f32[2,4,34,256]{3,2,1,0:T(8,128)S(1)}, f32[16,32,256]{2,1,0:T(8,128)S(1)...) custom-call(f32[4,4,32,256]{3,2,1,0:T(8,128)} %v_hbm.1, f32[4,4,2,256]{3,2,1,0:T(2,128)} %c_hbm.1, s32[4,4,8]{2,1,0:T(4,128)} %bitcast.17), custom_call_target="tpu_custom_call" | custom-call | bytes 557568 | tf_op jit(solution)/shard_map/pack_kernel/pallas_call | solution.py:350
  2.7 3.0 %collective-permute-start.1 = (f32[4,34,256]{2,1,0:T(8,128)S(1)}, f32[4,34,256]{2,1,0:T(8,128)S(1)}, u32[]{:S(2)}, u32[]{:S(2)}) collective-permute-start(f32[4,34,256]{2,1,0:T(8,128)S(1)} %get-tuple-element.74), channel_id=1, source_target_pairs={{0,8},{8,0},{16,24},{24,16},{1,9},{9,1},{17,25},{25,17},{2,10},{10... | collective-permute-start | bytes 417800 | tf_op jit(solution)/shard_map/ppermute | solution.py:341
  5.7 0.7 collective-permute-start
  6.4 6.0 %own_first_kernel.1 = (s32[45]{0:T(128)S(1)}, s32[47]{0:T(128)S(1)}, f32[16,32,256]{2,1,0:T(8,128)S(1)}, bf16[16,2,256,256]{3,2,1,0:T(8,128)(2,1)S(1)}, bf16[16,...) custom-call(s32[4,4,8]{2,1,0:T(4,128)S(1)} %get-tuple-element.31.pair_ref, ...), custom_call_target="tpu_custom_call" | custom-call | flops 201326592 | bytes 557568 | tf_op jit(solution)/shard_map/own_first_kernel/pallas_call | solution.py:350
  12.4 0.0 collective-permute-done.1
  12.4 0.0 collective-permute-done
  12.5 0.1 collective-permute-start.3
  12.6 0.7 collective-permute-start.2
  13.3 3.1 %inner_first_kernel.1 = (f32[16,32,256]{2,1,0:T(8,128)S(1)}, bf16[44,2,256,256]{3,2,1,0:T(8,128)(2,1)S(1)}) custom-call(s32[45]{0:T(128)S(1)} %get-tuple-element.35.items_ref.near_ref, f32[16,32,256]{2,1,0:T(8,128)S(1)} %get-tuple-element.38.sum_ref, bf16[16,64,256]{2,1,0:T(8,128)(2,1)S(1)} %get-tuple-element.39.parts_ref, ...), custom_call_target="tpu_custom_call" | custom-call | flops 528482304 | bytes 5800116 | tf_op jit(solution)/shard_map/inner_first_kernel/pallas_call | solution.py:350
  16.4 0.0 collective-permute-done.3
  16.4 0.0 collective-permute-done.2
  16.5 2.1 %cross_first_kernel.1 = (f32[16,32,256]{2,1,0:T(8,128)S(1)}, bf16[46,2,256,256]{3,2,1,0:T(8,128)(2,1)S(1)}) custom-call(s32[47]{0:T(128)S(1)} %get-tuple-element.34.items_ref.cross_ref, f32[16,32,256]{2,1,0:T(8,128)S(1)} %get-tuple-element.42.sum_ref, f32[4,34,256]{2,1,0:T(8,128)S(1)} %get-tuple-element.43.north_ref, ...), custom_call_target="tpu_custom_call" | custom-call | flops 553648128 | bytes 5415100 | tf_op jit(solution)/shard_map/cross_first_kernel/pallas_call | solution.py:350
  18.6 6.0 %collective-permute-start.5 = (f32[4,32,256]{2,1,0:T(8,128)S(1)}, f32[4,32,256]{2,1,0:T(8,128)S(1)}, u32[]{:S(2)}, u32[]{:S(2)}) collective-permute-start(f32[4,32,256]{2,1,0:T(8,128)S(1)} %get-tuple-element.62), channel_id=1, source_target_pairs={{0,8},{8,0},{16,24},{24,16},{1,9},{9,1},{17,25},{25,17},{2,10},{10... | collective-permute-start | bytes 393224 | tf_op jit(solution)/shard_map/ppermute | solution.py:341
  24.7 0.7 collective-permute-start.4
  25.4 2.9 %near_again_kernel.1 = (f32[16,32,256]{2,1,0:T(8,128)S(1)}, bf16[16,64,256]{2,1,0:T(8,128)(2,1)S(1)}) custom-call(s32[45]{0:T(128)S(1)} %get-tuple-element.35.items_ref.near_ref, f32[16,32,256]{2,1,0:T(8,128)S(1)} %get-tuple-element.47.v_ref.v1_ref, bf16[16,2,256,256]{3,2,1,0:T(8,128)(2,1)S(1)} %get-tuple-element.48.own_ref, ...), custom_call_target="tpu_custom_call" | custom-call | flops 729808896 | bytes 31981748 | tf_op jit(solution)/shard_map/near_again_kernel/pallas_call | solution.py:350
  28.3 0.0 collective-permute-done.5
  28.3 0.0 collective-permute-done.4
  28.4 16.3 %collective-permute-start.7 = (f32[6,32,256]{2,1,0:T(8,128)S(1)}, f32[6,32,256]{2,1,0:T(8,128)S(1)}, u32[]{:S(2)}, u32[]{:S(2)}) collective-permute-start(f32[6,32,256]{2,1,0:T(8,128)S(1)} %get-tuple-element.70), channel_id=1, source_target_pairs={{0,1},{1,0},{2,3},{3,2},{4,5},{5,4},{6,7},{7,6},{8,9},{9,8},{10,11... | collective-permute-start | bytes 589832 | tf_op jit(solution)/shard_map/ppermute | solution.py:341
  44.7 0.7 collective-permute-start.6
  45.4 1.9 %rest_again_kernel.1.sum_ref = f32[16,32,256]{2,1,0:T(8,128)S(1)} custom-call(s32[45]{0:T(128)S(1)} %get-tuple-element.35.items_ref.near_ref, s32[47]{0:T(128)S(1)} %get-tuple-element.34.items_ref.cross_ref, f32[16,32,256]{2,1,0:T(8,128)S(1)} %get-tuple-element.51.sum_ref, bf16[16,64,256]{2,1,0:T(8,128)(2,1)S(1)} %get-tuple-element.52.parts_ref, ...), custom_call_target="tpu_custom_call" | custom-call | flops 528482304 | bytes 49021296 | tf_op jit(solution)/shard_map/rest_again_kernel/pallas_call | solution.py:350
  47.2 0.0 collective-permute-done.7
  47.2 0.0 collective-permute-done.6
  47.3 1.4 %cross_again_kernel.1 = (f32[16,32,256]{2,1,0:T(8,128)S(1)}, f32[32,1,128]{2,1,0:T(1,128)S(1)}) custom-call(s32[47]{0:T(128)S(1)} %get-tuple-element.34.items_ref.cross_ref, f32[16,32,256]{2,1,0:T(8,128)S(1)} %rest_again_kernel.1.sum_ref, f32[6,32,256]{2,1,0:T(8,128)S(1)} %get-tuple-element.69.west_ref, f32[6,32,256]{2,1,0:T(8,128)S(1)} %get-tuple-element.68.east_ref, ...), custom_call_target="tpu_custom_call" | custom-call | flops 553648128 | bytes 26083516 | tf_op jit(solution)/shard_map/cross_again_kernel/pallas_call | solution.py:350
  48.7 21.4 %all_to_all.5.moments_ref = f32[32,1,128]{2,1,0:T(1,128)S(1)} all-to-all(f32[32,1,128]{2,1,0:T(1,128)S(1)} %get-tuple-element.56), channel_id=1, replica_groups=mesh['region'=4,'tile'=8] {'region','tile'}, dimensions={0} | all-to-all | bytes 32768 | tf_op jit(solution)/shard_map/all_to_all | solution.py:435
  70.1 1.3 %final_kernel.1 = (f32[16,32,256]{2,1,0:T(8,128)}, f32[16,32,256]{2,1,0:T(8,128)}) custom-call(f32[32,1,128]{2,1,0:T(1,128)S(1)} %all_to_all.5.moments_ref, f32[16,32,256]{2,1,0:T(8,128)S(1)} %get-tuple-element.32.v_ref.v0_ref, f32[16,32,256]{2,1,0:T(8,128)S(1)} %get-tuple-element.47.v_ref.v1_ref, f32[16,32,256]{2,1,0:T(8,128)S(1)} %get-tuple-element.57.v2_ref), custom_call_target="tpu_custom_call" | custom-call | bytes 1589248 | tf_op jit(solution)/shard_map/final_kernel/pallas_call | solution.py:350
  (12 shorter events, 0.3 us)
Async XLA Ops:
  2.7 9.7 %collective-permute-start.1 = (f32[4,34,256]{2,1,0:T(8,128)S(1)}, f32[4,34,256]{2,1,0:T(8,128)S(1)}, u32[]{:S(2)}, u32[]{:S(2)}) collective-permute-start(f32[4,34,256]{2,1,0:T(8,128)S(1)} %get-tuple-element.74), channel_id=1, source_target_pairs={{0,8},{8,0},{16,24},{24,16},{1,9},{9,1},{17,25},{25,17},{2,10},{10... | collective-permute-start | bytes 417800 | tf_op jit(solution)/shard_map/ppermute | solution.py:341
  5.7 6.7 %collective-permute-start = (f32[4,34,256]{2,1,0:T(8,128)S(1)}, f32[4,34,256]{2,1,0:T(8,128)S(1)}, u32[]{:S(2)}, u32[]{:S(2)}) collective-permute-start(f32[4,34,256]{2,1,0:T(8,128)S(1)} %get-tuple-element.75), channel_id=1, source_target_pairs={{8,16},{16,8},{9,17},{17,9},{10,18},{18,10},{11,19},{19,11},{12,20... | collective-permute-start | bytes 417800 | tf_op jit(solution)/shard_map/ppermute | solution.py:342
  12.5 3.9 %collective-permute-start.3 = (f32[6,34,256]{2,1,0:T(8,128)S(1)}, f32[6,34,256]{2,1,0:T(8,128)S(1)}, u32[]{:S(2)}, u32[]{:S(2)}) collective-permute-start(f32[6,34,256]{2,1,0:T(8,128)S(1)} %get-tuple-element.66), channel_id=1, source_target_pairs={{0,1},{1,0},{2,3},{3,2},{4,5},{5,4},{6,7},{7,6},{8,9},{9,8},{10,11... | collective-permute-start | bytes 626696 | tf_op jit(solution)/shard_map/ppermute | solution.py:341
  12.6 3.8 %collective-permute-start.2 = (f32[6,34,256]{2,1,0:T(8,128)S(1)}, f32[6,34,256]{2,1,0:T(8,128)S(1)}, u32[]{:S(2)}, u32[]{:S(2)}) collective-permute-start(f32[6,34,256]{2,1,0:T(8,128)S(1)} %get-tuple-element.67), channel_id=1, source_target_pairs={{1,2},{2,1},{3,4},{4,3},{5,6},{6,5},{9,10},{10,9},{11,12},{12,11},... | collective-permute-start | bytes 626696 | tf_op jit(solution)/shard_map/ppermute | solution.py:342
  18.6 9.6 %collective-permute-start.5 = (f32[4,32,256]{2,1,0:T(8,128)S(1)}, f32[4,32,256]{2,1,0:T(8,128)S(1)}, u32[]{:S(2)}, u32[]{:S(2)}) collective-permute-start(f32[4,32,256]{2,1,0:T(8,128)S(1)} %get-tuple-element.62), channel_id=1, source_target_pairs={{0,8},{8,0},{16,24},{24,16},{1,9},{9,1},{17,25},{25,17},{2,10},{10... | collective-permute-start | bytes 393224 | tf_op jit(solution)/shard_map/ppermute | solution.py:341
  24.7 3.6 %collective-permute-start.4 = (f32[4,32,256]{2,1,0:T(8,128)S(1)}, f32[4,32,256]{2,1,0:T(8,128)S(1)}, u32[]{:S(2)}, u32[]{:S(2)}) collective-permute-start(f32[4,32,256]{2,1,0:T(8,128)S(1)} %get-tuple-element.63), channel_id=1, source_target_pairs={{8,16},{16,8},{9,17},{17,9},{10,18},{18,10},{11,19},{19,11},{12,20... | collective-permute-start | bytes 393224 | tf_op jit(solution)/shard_map/ppermute | solution.py:342
  28.4 18.8 %collective-permute-start.7 = (f32[6,32,256]{2,1,0:T(8,128)S(1)}, f32[6,32,256]{2,1,0:T(8,128)S(1)}, u32[]{:S(2)}, u32[]{:S(2)}) collective-permute-start(f32[6,32,256]{2,1,0:T(8,128)S(1)} %get-tuple-element.70), channel_id=1, source_target_pairs={{0,1},{1,0},{2,3},{3,2},{4,5},{5,4},{6,7},{7,6},{8,9},{9,8},{10,11... | collective-permute-start | bytes 589832 | tf_op jit(solution)/shard_map/ppermute | solution.py:341
  44.7 2.5 %collective-permute-start.6 = (f32[6,32,256]{2,1,0:T(8,128)S(1)}, f32[6,32,256]{2,1,0:T(8,128)S(1)}, u32[]{:S(2)}, u32[]{:S(2)}) collective-permute-start(f32[6,32,256]{2,1,0:T(8,128)S(1)} %get-tuple-element.71), channel_id=1, source_target_pairs={{1,2},{2,1},{3,4},{4,3},{5,6},{6,5},{9,10},{10,9},{11,12},{12,11},... | collective-permute-start | bytes 589832 | tf_op jit(solution)/shard_map/ppermute | solution.py:342

commit v2 on v1

--- a/solution.py
+++ b/solution.py
@@ -16,6 +16,7 @@
 WEIGHT = 4.0 * 2.0**-EDGE / EDGE**5
 STRIP = 64
 LONG_TURN_LOG2 = 3
+OWN_TURN_LOG2 = 2
 VMEM_LIMIT = 10 * 1024 * 1024
 
 
@@ -37,17 +38,17 @@
     return jnp.transpose(jnp.broadcast_to(row, (lanes, row.shape[1])))
 
 
-def make_tile(keep_ref, slot, spread_ref, down, points_ref, along, shift_a, shift_b):
+def make_tile(keep_ref, slot, down_x, down_y, points_ref, along, shift_a, shift_b):
     points = keep_ref.shape[2]
-    lanes = spread_ref.shape[3]
+    lanes = down_x.shape[1]
     row_x = points_ref[along, 0:1] - shift_a
     row_y = points_ref[along, 1:2] - shift_b
     for start in range(0, points, STRIP):
         rows = slice(start, start + STRIP)
         for left in range(0, points, lanes):
             cols = slice(left, left + lanes)
-            gap_x = spread_ref[down, 0, rows] - row_x[:, cols]
-            gap_y = spread_ref[down, 1, rows] - row_y[:, cols]
+            gap_x = down_x[rows] - row_x[:, cols]
+            gap_y = down_y[rows] - row_y[:, cols]
             square = jnp.maximum(gap_x * gap_x + gap_y * gap_y, 1e-30)
             rest = jnp.maximum(EDGE - square * lax.rsqrt(square), 0.0)
             rest2 = rest * rest
@@ -70,15 +71,16 @@
     parts_ref[at, rhs : 2 * rhs] = lo
 
 
-def in_turns(count, step):
-    turns = lax.shift_right_logical(count + 1, 1)
+def in_turns(count, step, log2=2):
+    whole = lax.shift_right_logical(count, log2)
 
     def one_turn(turn, carry):
-        step(2 * turn)
-        step(2 * turn + 1)
+        for n in range(1 << log2):
+            step((turn << log2) + n)
         return carry
 
-    lax.fori_loop(0, turns, one_turn, 0)
+    lax.fori_loop(0, whole, one_turn, 0)
+    lax.fori_loop(whole << log2, count, lambda n, c: (step(n), c)[1], 0)
 
 
 def only_use(first, last, kept_ref, use):
@@ -203,16 +205,12 @@
         out_ref[at] = NUGGET * v_ref[at]
         scaled = c_ref[at] * UNIT
         points_ref[at] = scaled
+        down = [across_lanes(scaled[axis : axis + 1], lanes) for axis in range(2)]
+        make_tile(kept_ref, at, *down, points_ref, at, 0.0, 0.0)
         for axis in range(2):
-            spread_ref[at, axis] = across_lanes(scaled[axis : axis + 1], lanes)
-        make_tile(kept_ref, at, spread_ref, at, points_ref, at, 0.0, 0.0)
-
-    def one_pair(turn, carry):
-        one(2 * turn)
-        one(2 * turn + 1)
-        return carry
-
-    lax.fori_loop(0, rows * cols // 2, one_pair, 0)
+            spread_ref[at, axis] = down[axis]
+
+    in_turns(jnp.int32(rows * cols), one, OWN_TURN_LOG2)
     only_use(0, jnp.int32(rows * cols), kept_ref, functools.partial(use_own, out_ref, parts_ref))
     list_items(near_ref, inner_candidates(rows, cols), pair_ref)
     in_rows, in_columns = cross_candidates(rows, cols)
@@ -225,7 +223,7 @@
     def make(n):
         code = items_ref[n + 1]
         own, other = item_blocks(code)
-        make_tile(kept_ref, n, spread_ref, other, points_ref, own, *item_shifts(code))
+        make_tile(kept_ref, n, spread_ref.at[other, 0], spread_ref.at[other, 1], points_ref, own, *item_shifts(code))
 
     in_turns(items_ref[0], make)
     only_use(0, items_ref[0], kept_ref, functools.partial(use_pair, out_ref, parts_ref, items_ref))
@@ -254,7 +252,7 @@
     def make(n):
         code = items_ref[n + 1]
         own, other = item_blocks(code)
-        make_tile(kept_ref, n, spread_ref, own, points_ref, other, *item_shifts(code))
+        make_tile(kept_ref, n, spread_ref.at[own, 0], spread_ref.at[own, 1], points_ref, other, *item_shifts(code))
 
     in_turns(items_ref[0], make)
     only_use(0, items_ref[0], kept_ref, functools.partial(use_cross, out_ref, parts_ref, items_ref))

time: 72.4 us -> 71.9 us (level)
  starting transfers between devices: 28.1 us -> 13.2 us
  blocking collectives: 21.4 us -> 33.7 us
  Pallas kernels: 20.7 us -> 22.7 us
    ppermute x4, starting transfers between devices: 25.4 us -> 10.6 us  [swapped(): got_up = lax.ppermute(jnp.where(even, last, first), axis, swap_up)]
    all_to_all x1, blocking collectives: 21.4 us -> 33.7 us  [per_device(): moments = lax.all_to_all(moments, ('region', 'tile'), 0, 0)]
    pallas_call x8, Pallas kernels: 20.7 us -> 22.7 us  [on_device(): pl.pallas_call(kernel, out_shape=tuple(outputs), in_specs=[smem if listed...]
  transfers between devices with their start and end apart: 8 -> 8, of which waited for: 0 -> 0; matrix products, arithmetic and copies ran while one was open for 0% -> 0% of each run, Pallas kernels for 19% -> 21%
where the time goes in v2:
time: 71.9 us; the launch traced here: 70.8 us
  blocking collectives  33.7 us (47%)
  Pallas kernels  22.7 us (32%)
  starting transfers between devices  13.2 us (18%)
  between operations  0.88 us (1%)
    all_to_all x1, blocking collectives, per_device(): moments = lax.all_to_all(moments, ('region', 'tile'), 0, 0)  33.7 us
    pallas_call x8, Pallas kernels, on_device(): pl.pallas_call(kernel, out_shape=tuple(outputs), in_specs=[smem if listed...  22.7 us
    ppermute x4, starting transfers between devices, swapped(): got_up = lax.ppermute(jnp.where(even, last, first), axis, swap_up)  10.6 us
    ppermute x4, starting transfers between devices, swapped(): got_down = lax.ppermute(jnp.where(even, first, last), axis, swap_down)  2.65 us
  transfers between devices with their start and end apart: 8, of which 0 were waited for; matrix products, arithmetic and copies ran while one was open for 0% of the time, Pallas kernels for 21%

profile of v2, /device:TPU:0, one launch (start us, length us, event | category | flops | bytes accessed | tf_op | source)
XLA Modules:
  0.0 70.8 jit_solution(3708349680274791853)
XLA Ops:
  0.6 2.0 %pack_kernel.1 = (f32[4,34,256]{2,1,0:T(8,128)S(1)}, f32[4,34,256]{2,1,0:T(8,128)S(1)}, f32[2,4,34,256]{3,2,1,0:T(8,128)S(1)}, f32[16,32,256]{2,1,0:T(8,128)S(1)...) custom-call(f32[4,4,32,256]{3,2,1,0:T(8,128)} %v_hbm.1, f32[4,4,2,256]{3,2,1,0:T(2,128)} %c_hbm.1, s32[4,4,8]{2,1,0:T(4,128)} %bitcast.17), custom_call_target="tpu_custom_call" | custom-call | bytes 557568 | tf_op jit(solution)/shard_map/pack_kernel/pallas_call | solution.py:348
  2.7 3.0 %collective-permute-start.1 = (f32[4,34,256]{2,1,0:T(8,128)S(1)}, f32[4,34,256]{2,1,0:T(8,128)S(1)}, u32[]{:S(2)}, u32[]{:S(2)}) collective-permute-start(f32[4,34,256]{2,1,0:T(8,128)S(1)} %get-tuple-element.74), channel_id=1, source_target_pairs={{0,8},{8,0},{16,24},{24,16},{1,9},{9,1},{17,25},{25,17},{2,10},{10... | collective-permute-start | bytes 417800 | tf_op jit(solution)/shard_map/ppermute | solution.py:339
  5.7 0.7 collective-permute-start
  6.4 5.6 %own_first_kernel.1 = (s32[45]{0:T(128)S(1)}, s32[47]{0:T(128)S(1)}, f32[16,32,256]{2,1,0:T(8,128)S(1)}, bf16[16,2,256,256]{3,2,1,0:T(8,128)(2,1)S(1)}, bf16[16,...) custom-call(s32[4,4,8]{2,1,0:T(4,128)S(1)} %get-tuple-element.31.pair_ref, ...), custom_call_target="tpu_custom_call" | custom-call | flops 201326592 | bytes 557568 | tf_op jit(solution)/shard_map/own_first_kernel/pallas_call | solution.py:348
  12.0 0.0 collective-permute-done.1
  12.0 0.0 collective-permute-done
  12.1 0.1 collective-permute-start.3
  12.2 0.7 collective-permute-start.2
  12.9 4.0 %inner_first_kernel.1 = (f32[16,32,256]{2,1,0:T(8,128)S(1)}, bf16[44,2,256,256]{3,2,1,0:T(8,128)(2,1)S(1)}) custom-call(s32[45]{0:T(128)S(1)} %get-tuple-element.35.items_ref.near_ref, f32[16,32,256]{2,1,0:T(8,128)S(1)} %get-tuple-element.38.sum_ref, bf16[16,64,256]{2,1,0:T(8,128)(2,1)S(1)} %get-tuple-element.39.parts_ref, ...), custom_call_target="tpu_custom_call" | custom-call | flops 528482304 | bytes 5800116 | tf_op jit(solution)/shard_map/inner_first_kernel/pallas_call | solution.py:348
  16.9 0.0 collective-permute-done.3
  16.9 0.0 collective-permute-done.2
  17.0 2.7 %cross_first_kernel.1 = (f32[16,32,256]{2,1,0:T(8,128)S(1)}, bf16[46,2,256,256]{3,2,1,0:T(8,128)(2,1)S(1)}) custom-call(s32[47]{0:T(128)S(1)} %get-tuple-element.34.items_ref.cross_ref, f32[16,32,256]{2,1,0:T(8,128)S(1)} %get-tuple-element.42.sum_ref, f32[4,34,256]{2,1,0:T(8,128)S(1)} %get-tuple-element.43.north_ref, ...), custom_call_target="tpu_custom_call" | custom-call | flops 553648128 | bytes 5415100 | tf_op jit(solution)/shard_map/cross_first_kernel/pallas_call | solution.py:348
  19.7 3.0 %collective-permute-start.5 = (f32[4,32,256]{2,1,0:T(8,128)S(1)}, f32[4,32,256]{2,1,0:T(8,128)S(1)}, u32[]{:S(2)}, u32[]{:S(2)}) collective-permute-start(f32[4,32,256]{2,1,0:T(8,128)S(1)} %get-tuple-element.62), channel_id=1, source_target_pairs={{0,8},{8,0},{16,24},{24,16},{1,9},{9,1},{17,25},{25,17},{2,10},{10... | collective-permute-start | bytes 393224 | tf_op jit(solution)/shard_map/ppermute | solution.py:339
  22.7 0.7 collective-permute-start.4
  23.4 3.2 %near_again_kernel.1 = (f32[16,32,256]{2,1,0:T(8,128)S(1)}, bf16[16,64,256]{2,1,0:T(8,128)(2,1)S(1)}) custom-call(s32[45]{0:T(128)S(1)} %get-tuple-element.35.items_ref.near_ref, f32[16,32,256]{2,1,0:T(8,128)S(1)} %get-tuple-element.47.v_ref.v1_ref, bf16[16,2,256,256]{3,2,1,0:T(8,128)(2,1)S(1)} %get-tuple-element.48.own_ref, ...), custom_call_target="tpu_custom_call" | custom-call | flops 729808896 | bytes 31981748 | tf_op jit(solution)/shard_map/near_again_kernel/pallas_call | solution.py:348
  26.6 0.0 collective-permute-done.5
  26.6 0.0 collective-permute-done.4
  26.7 4.4 %collective-permute-start.7 = (f32[6,32,256]{2,1,0:T(8,128)S(1)}, f32[6,32,256]{2,1,0:T(8,128)S(1)}, u32[]{:S(2)}, u32[]{:S(2)}) collective-permute-start(f32[6,32,256]{2,1,0:T(8,128)S(1)} %get-tuple-element.70), channel_id=1, source_target_pairs={{0,1},{1,0},{2,3},{3,2},{4,5},{5,4},{6,7},{7,6},{8,9},{9,8},{10,11... | collective-permute-start | bytes 589832 | tf_op jit(solution)/shard_map/ppermute | solution.py:339
  31.2 0.7 collective-permute-start.6
  31.8 2.1 %rest_again_kernel.1.sum_ref = f32[16,32,256]{2,1,0:T(8,128)S(1)} custom-call(s32[45]{0:T(128)S(1)} %get-tuple-element.35.items_ref.near_ref, s32[47]{0:T(128)S(1)} %get-tuple-element.34.items_ref.cross_ref, f32[16,32,256]{2,1,0:T(8,128)S(1)} %get-tuple-element.51.sum_ref, bf16[16,64,256]{2,1,0:T(8,128)(2,1)S(1)} %get-tuple-element.52.parts_ref, ...), custom_call_target="tpu_custom_call" | custom-call | flops 528482304 | bytes 49021296 | tf_op jit(solution)/shard_map/rest_again_kernel/pallas_call | solution.py:348
  34.0 0.0 collective-permute-done.7
  34.0 0.0 collective-permute-done.6
  34.0 1.8 %cross_again_kernel.1 = (f32[16,32,256]{2,1,0:T(8,128)S(1)}, f32[32,1,128]{2,1,0:T(1,128)S(1)}) custom-call(s32[47]{0:T(128)S(1)} %get-tuple-element.34.items_ref.cross_ref, f32[16,32,256]{2,1,0:T(8,128)S(1)} %rest_again_kernel.1.sum_ref, f32[6,32,256]{2,1,0:T(8,128)S(1)} %get-tuple-element.69.west_ref, f32[6,32,256]{2,1,0:T(8,128)S(1)} %get-tuple-element.68.east_ref, ...), custom_call_target="tpu_custom_call" | custom-call | flops 553648128 | bytes 26083516 | tf_op jit(solution)/shard_map/cross_again_kernel/pallas_call | solution.py:348
  35.8 33.7 %all_to_all.5.moments_ref = f32[32,1,128]{2,1,0:T(1,128)S(1)} all-to-all(f32[32,1,128]{2,1,0:T(1,128)S(1)} %get-tuple-element.56), channel_id=1, replica_groups=mesh['region'=4,'tile'=8] {'region','tile'}, dimensions={0} | all-to-all | bytes 32768 | tf_op jit(solution)/shard_map/all_to_all | solution.py:433
  69.5 1.3 %final_kernel.1 = (f32[16,32,256]{2,1,0:T(8,128)}, f32[16,32,256]{2,1,0:T(8,128)}) custom-call(f32[32,1,128]{2,1,0:T(1,128)S(1)} %all_to_all.5.moments_ref, f32[16,32,256]{2,1,0:T(8,128)S(1)} %get-tuple-element.32.v_ref.v0_ref, f32[16,32,256]{2,1,0:T(8,128)S(1)} %get-tuple-element.47.v_ref.v1_ref, f32[16,32,256]{2,1,0:T(8,128)S(1)} %get-tuple-element.57.v2_ref), custom_call_target="tpu_custom_call" | custom-call | bytes 1589248 | tf_op jit(solution)/shard_map/final_kernel/pallas_call | solution.py:348
  (12 shorter events, 0.3 us)
Async XLA Ops:
  2.7 9.3 %collective-permute-start.1 = (f32[4,34,256]{2,1,0:T(8,128)S(1)}, f32[4,34,256]{2,1,0:T(8,128)S(1)}, u32[]{:S(2)}, u32[]{:S(2)}) collective-permute-start(f32[4,34,256]{2,1,0:T(8,128)S(1)} %get-tuple-element.74), channel_id=1, source_target_pairs={{0,8},{8,0},{16,24},{24,16},{1,9},{9,1},{17,25},{25,17},{2,10},{10... | collective-permute-start | bytes 417800 | tf_op jit(solution)/shard_map/ppermute | solution.py:339
  5.7 6.3 %collective-permute-start = (f32[4,34,256]{2,1,0:T(8,128)S(1)}, f32[4,34,256]{2,1,0:T(8,128)S(1)}, u32[]{:S(2)}, u32[]{:S(2)}) collective-permute-start(f32[4,34,256]{2,1,0:T(8,128)S(1)} %get-tuple-element.75), channel_id=1, source_target_pairs={{8,16},{16,8},{9,17},{17,9},{10,18},{18,10},{11,19},{19,11},{12,20... | collective-permute-start | bytes 417800 | tf_op jit(solution)/shard_map/ppermute | solution.py:340
  12.1 4.8 %collective-permute-start.3 = (f32[6,34,256]{2,1,0:T(8,128)S(1)}, f32[6,34,256]{2,1,0:T(8,128)S(1)}, u32[]{:S(2)}, u32[]{:S(2)}) collective-permute-start(f32[6,34,256]{2,1,0:T(8,128)S(1)} %get-tuple-element.66), channel_id=1, source_target_pairs={{0,1},{1,0},{2,3},{3,2},{4,5},{5,4},{6,7},{7,6},{8,9},{9,8},{10,11... | collective-permute-start | bytes 626696 | tf_op jit(solution)/shard_map/ppermute | solution.py:339
  12.2 4.7 %collective-permute-start.2 = (f32[6,34,256]{2,1,0:T(8,128)S(1)}, f32[6,34,256]{2,1,0:T(8,128)S(1)}, u32[]{:S(2)}, u32[]{:S(2)}) collective-permute-start(f32[6,34,256]{2,1,0:T(8,128)S(1)} %get-tuple-element.67), channel_id=1, source_target_pairs={{1,2},{2,1},{3,4},{4,3},{5,6},{6,5},{9,10},{10,9},{11,12},{12,11},... | collective-permute-start | bytes 626696 | tf_op jit(solution)/shard_map/ppermute | solution.py:340
  19.7 6.9 %collective-permute-start.5 = (f32[4,32,256]{2,1,0:T(8,128)S(1)}, f32[4,32,256]{2,1,0:T(8,128)S(1)}, u32[]{:S(2)}, u32[]{:S(2)}) collective-permute-start(f32[4,32,256]{2,1,0:T(8,128)S(1)} %get-tuple-element.62), channel_id=1, source_target_pairs={{0,8},{8,0},{16,24},{24,16},{1,9},{9,1},{17,25},{25,17},{2,10},{10... | collective-permute-start | bytes 393224 | tf_op jit(solution)/shard_map/ppermute | solution.py:339
  22.7 3.9 %collective-permute-start.4 = (f32[4,32,256]{2,1,0:T(8,128)S(1)}, f32[4,32,256]{2,1,0:T(8,128)S(1)}, u32[]{:S(2)}, u32[]{:S(2)}) collective-permute-start(f32[4,32,256]{2,1,0:T(8,128)S(1)} %get-tuple-element.63), channel_id=1, source_target_pairs={{8,16},{16,8},{9,17},{17,9},{10,18},{18,10},{11,19},{19,11},{12,20... | collective-permute-start | bytes 393224 | tf_op jit(solution)/shard_map/ppermute | solution.py:340
  26.7 7.2 %collective-permute-start.7 = (f32[6,32,256]{2,1,0:T(8,128)S(1)}, f32[6,32,256]{2,1,0:T(8,128)S(1)}, u32[]{:S(2)}, u32[]{:S(2)}) collective-permute-start(f32[6,32,256]{2,1,0:T(8,128)S(1)} %get-tuple-element.70), channel_id=1, source_target_pairs={{0,1},{1,0},{2,3},{3,2},{4,5},{5,4},{6,7},{7,6},{8,9},{9,8},{10,11... | collective-permute-start | bytes 589832 | tf_op jit(solution)/shard_map/ppermute | solution.py:339
  31.2 2.8 %collective-permute-start.6 = (f32[6,32,256]{2,1,0:T(8,128)S(1)}, f32[6,32,256]{2,1,0:T(8,128)S(1)}, u32[]{:S(2)}, u32[]{:S(2)}) collective-permute-start(f32[6,32,256]{2,1,0:T(8,128)S(1)} %get-tuple-element.71), channel_id=1, source_target_pairs={{1,2},{2,1},{3,4},{4,3},{5,6},{6,5},{9,10},{10,9},{11,12},{12,11},... | collective-permute-start | bytes 589832 | tf_op jit(solution)/shard_map/ppermute | solution.py:340

commit v3 on v2

--- a/solution.py
+++ b/solution.py
@@ -14,9 +14,7 @@
 UNIT = 1.4426950408889634 / LENGTH_SCALE
 EDGE = UNIT * TAPER_RANGE
 WEIGHT = 4.0 * 2.0**-EDGE / EDGE**5
-STRIP = 64
-LONG_TURN_LOG2 = 3
-OWN_TURN_LOG2 = 2
+CHUNK = 128
 VMEM_LIMIT = 10 * 1024 * 1024
 
 
@@ -38,23 +36,31 @@
     return jnp.transpose(jnp.broadcast_to(row, (lanes, row.shape[1])))
 
 
-def make_tile(keep_ref, slot, down_x, down_y, points_ref, along, shift_a, shift_b):
-    points = keep_ref.shape[2]
+def tile_rows(rows, down_x, down_y, points_ref, along, shift_a, shift_b):
+    points = points_ref.shape[2]
     lanes = down_x.shape[1]
     row_x = points_ref[along, 0:1] - shift_a
     row_y = points_ref[along, 1:2] - shift_b
-    for start in range(0, points, STRIP):
-        rows = slice(start, start + STRIP)
-        for left in range(0, points, lanes):
-            cols = slice(left, left + lanes)
-            gap_x = down_x[rows] - row_x[:, cols]
-            gap_y = down_y[rows] - row_y[:, cols]
-            square = jnp.maximum(gap_x * gap_x + gap_y * gap_y, 1e-30)
-            rest = jnp.maximum(EDGE - square * lax.rsqrt(square), 0.0)
-            rest2 = rest * rest
-            cov = (jnp.exp2(rest) * (rest2 * rest2)) * (1.25 * EDGE - rest)
-            for part, values in enumerate(split_hi_lo(cov)):
-                keep_ref[slot, part, rows, cols] = values
+    halves = []
+    for left in range(0, points, lanes):
+        cols = slice(left, left + lanes)
+        gap_x = down_x[rows] - row_x[:, cols]
+        gap_y = down_y[rows] - row_y[:, cols]
+        square = jnp.maximum(gap_x * gap_x + gap_y * gap_y, 1e-30)
+        rest = jnp.maximum(EDGE - square * lax.rsqrt(square), 0.0)
+        rest2 = rest * rest
+        halves.append((jnp.exp2(rest) * (rest2 * rest2)) * (1.25 * EDGE - rest))
+    return split_hi_lo(jnp.concatenate(halves, axis=1))
+
+
+def make_tile(keep_ref, slot, down_x, down_y, points_ref, along, shift_a, shift_b, use):
+    points = keep_ref.shape[2]
+    for start in range(0, points, CHUNK):
+        rows = slice(start, start + CHUNK)
+        hi, lo = tile_rows(rows, down_x, down_y, points_ref, along, shift_a, shift_b)
+        keep_ref[slot, 0, rows] = hi
+        keep_ref[slot, 1, rows] = lo
+        use(hi, lo, rows)
 
 
 def product(dot, parts_ref, at, high, low):
@@ -71,26 +77,21 @@
     parts_ref[at, rhs : 2 * rhs] = lo
 
 
-def in_turns(count, step, log2=2):
-    whole = lax.shift_right_logical(count, log2)
-
-    def one_turn(turn, carry):
-        for n in range(1 << log2):
-            step((turn << log2) + n)
-        return carry
-
-    lax.fori_loop(0, whole, one_turn, 0)
-    lax.fori_loop(whole << log2, count, lambda n, c: (step(n), c)[1], 0)
+def in_turns(first, last, step, log2s=(3, 2, 1, 0)):
+    for log2 in log2s:
+        turns = lax.shift_right_logical(last - first, log2)
+
+        def one_turn(turn, carry, first=first, log2=log2):
+            for n in range(1 << log2):
+                step(first + (turn << log2) + n)
+            return carry
+
+        lax.fori_loop(0, turns, one_turn, 0)
+        first = first + (turns << log2)
 
 
 def only_use(first, last, kept_ref, use):
-    def one_turn(start, length):
-        for n in range(length):
-            use(kept_ref[start + n, 0], kept_ref[start + n, 1], start + n)
-
-    whole = lax.shift_right_logical(last - first, LONG_TURN_LOG2)
-    lax.fori_loop(0, whole, lambda turn, c: (one_turn(first + (turn << LONG_TURN_LOG2), 1 << LONG_TURN_LOG2), c)[1], 0)
-    lax.fori_loop(first + (whole << LONG_TURN_LOG2), last, lambda n, c: (one_turn(n, 1), c)[1], 0)
+    in_turns(first, last, lambda n: use(kept_ref[n, 0], kept_ref[n, 1], n))
 
 
 def item_code(own, other, shift_a, shift_b):
@@ -202,16 +203,22 @@
 
     def one(at):
         store_parts(parts_ref, at, v_ref[at])
-        out_ref[at] = NUGGET * v_ref[at]
         scaled = c_ref[at] * UNIT
         points_ref[at] = scaled
         down = [across_lanes(scaled[axis : axis + 1], lanes) for axis in range(2)]
-        make_tile(kept_ref, at, *down, points_ref, at, 0.0, 0.0)
+        rhs = out_ref.shape[1]
+        total = [NUGGET * v_ref[at]]
+
+        def use(hi, lo, rows):
+            both = dot_nn(parts_ref[at, :, rows], hi)
+            total[0] = total[0] + (both[:rhs] + both[rhs:] + dot_nn(parts_ref[at, 0:rhs, rows], lo))
+
+        make_tile(kept_ref, at, *down, points_ref, at, 0.0, 0.0, use)
+        out_ref[at] = total[0]
         for axis in range(2):
             spread_ref[at, axis] = down[axis]
 
-    in_turns(jnp.int32(rows * cols), one, OWN_TURN_LOG2)
-    only_use(0, jnp.int32(rows * cols), kept_ref, functools.partial(use_own, out_ref, parts_ref))
+    in_turns(0, jnp.int32(rows * cols), one)
     list_items(near_ref, inner_candidates(rows, cols), pair_ref)
     in_rows, in_columns = cross_candidates(rows, cols)
     list_items(cross_ref, in_rows, pair_ref, in_columns)
@@ -223,10 +230,21 @@
     def make(n):
         code = items_ref[n + 1]
         own, other = item_blocks(code)
-        make_tile(kept_ref, n, spread_ref.at[other, 0], spread_ref.at[other, 1], points_ref, own, *item_shifts(code))
-
-    in_turns(items_ref[0], make)
-    only_use(0, items_ref[0], kept_ref, functools.partial(use_pair, out_ref, parts_ref, items_ref))
+        rhs = out_ref.shape[1]
+        total = [jnp.zeros(out_ref.shape[1:], jnp.float32)]
+
+        def use(hi, lo, rows):
+            both = dot_nn(parts_ref[other, :, rows], hi)
+            total[0] = total[0] + (both[:rhs] + both[rhs:] + dot_nn(parts_ref[other, 0:rhs, rows], lo))
+            back = dot_nt(parts_ref[own], hi)
+            out_ref[other, :, rows] += back[:rhs] + back[rhs:] + dot_nt(parts_ref[own, 0:rhs], lo)
+
+        make_tile(
+            kept_ref, n, spread_ref.at[other, 0], spread_ref.at[other, 1], points_ref, own, *item_shifts(code), use
+        )
+        out_ref[own] += total[0]
+
+    in_turns(0, items_ref[0], make)
 
 
 def take_round(round_refs, rhs, parts_ref, points_ref=None, start=0):
@@ -252,10 +270,17 @@
     def make(n):
         code = items_ref[n + 1]
         own, other = item_blocks(code)
-        make_tile(kept_ref, n, spread_ref.at[own, 0], spread_ref.at[own, 1], points_ref, other, *item_shifts(code))
-
-    in_turns(items_ref[0], make)
-    only_use(0, items_ref[0], kept_ref, functools.partial(use_cross, out_ref, parts_ref, items_ref))
+        rhs = out_ref.shape[1]
+
+        def use(hi, lo, rows):
+            both = dot_nt(parts_ref[other], hi)
+            out_ref[own, :, rows] += both[:rhs] + both[rhs:] + dot_nt(parts_ref[other, 0:rhs], lo)
+
+        make_tile(
+            kept_ref, n, spread_ref.at[own, 0], spread_ref.at[own, 1], points_ref, other, *item_shifts(code), use
+        )
+
+    in_turns(0, items_ref[0], make)
 
 
 def first_share(count):

time: 71.9 us -> 61.8 us (0.86)
  blocking collectives: 33.7 us -> 25.5 us
  Pallas kernels: 22.7 us -> 17.3 us
  starting transfers between devices: 13.2 us -> 16.8 us
    all_to_all x1, blocking collectives: 33.7 us -> 25.5 us  [per_device(): moments = lax.all_to_all(moments, ('region', 'tile'), 0, 0)]
    pallas_call x8, Pallas kernels: 22.7 us -> 17.3 us  [on_device(): pl.pallas_call(kernel, out_shape=tuple(outputs), in_specs=[smem if listed...]
    ppermute x4, starting transfers between devices: 10.6 us -> 14.1 us  [swapped(): got_up = lax.ppermute(jnp.where(even, last, first), axis, swap_up)]
  transfers between devices with their start and end apart: 8 -> 8, of which waited for: 0 -> 1; matrix products, arithmetic and copies ran while one was open for 0% -> 0% of each run, Pallas kernels for 21% -> 18%
where the time goes in v3:
time: 61.8 us; the launch traced here: 60.8 us
  blocking collectives  25.5 us (41%)
  Pallas kernels  17.3 us (28%)
  starting transfers between devices  16.8 us (27%)
  between operations  0.87 us (1%)
    all_to_all x1, blocking collectives, per_device(): moments = lax.all_to_all(moments, ('region', 'tile'), 0, 0)  25.5 us
    pallas_call x8, Pallas kernels, on_device(): pl.pallas_call(kernel, out_shape=tuple(outputs), in_specs=[smem if listed...  17.3 us
    ppermute x4, starting transfers between devices, swapped(): got_up = lax.ppermute(jnp.where(even, last, first), axis, swap_up)  14.1 us
    ppermute x4, starting transfers between devices, swapped(): got_down = lax.ppermute(jnp.where(even, first, last), axis, swap_down)  2.65 us
  transfers between devices with their start and end apart: 8, of which 1 were waited for; matrix products, arithmetic and copies ran while one was open for 0% of the time, Pallas kernels for 18%

profile of v3, /device:TPU:0, one launch (start us, length us, event | category | flops | bytes accessed | tf_op | source)
XLA Modules:
  0.0 60.8 jit_solution(13986679295532164042)
XLA Ops:
  0.6 2.0 %pack_kernel.1 = (f32[4,34,256]{2,1,0:T(8,128)S(1)}, f32[4,34,256]{2,1,0:T(8,128)S(1)}, f32[2,4,34,256]{3,2,1,0:T(8,128)S(1)}, f32[16,32,256]{2,1,0:T(8,128)S(1)...) custom-call(f32[4,4,32,256]{3,2,1,0:T(8,128)} %v_hbm.1, f32[4,4,2,256]{3,2,1,0:T(2,128)} %c_hbm.1, s32[4,4,8]{2,1,0:T(4,128)} %bitcast.17), custom_call_target="tpu_custom_call" | custom-call | bytes 557568 | tf_op jit(solution)/shard_map/pack_kernel/pallas_call | solution.py:373
  2.7 3.0 %collective-permute-start.1 = (f32[4,34,256]{2,1,0:T(8,128)S(1)}, f32[4,34,256]{2,1,0:T(8,128)S(1)}, u32[]{:S(2)}, u32[]{:S(2)}) collective-permute-start(f32[4,34,256]{2,1,0:T(8,128)S(1)} %get-tuple-element.74), channel_id=1, source_target_pairs={{0,8},{8,0},{16,24},{24,16},{1,9},{9,1},{17,25},{25,17},{2,10},{10... | collective-permute-start | bytes 417800 | tf_op jit(solution)/shard_map/ppermute | solution.py:364
  5.7 0.7 %collective-permute-start = (f32[4,34,256]{2,1,0:T(8,128)S(1)}, f32[4,34,256]{2,1,0:T(8,128)S(1)}, u32[]{:S(2)}, u32[]{:S(2)}) collective-permute-start(f32[4,34,256]{2,1,0:T(8,128)S(1)} %get-tuple-element.75), channel_id=1, source_target_pairs={{8,16},{16,8},{9,17},{17,9},{10,18},{18,10},{11,19},{19,11},{12,20... | collective-permute-start | bytes 417800 | tf_op jit(solution)/shard_map/ppermute | solution.py:365
  6.4 5.1 %own_first_kernel.1 = (s32[45]{0:T(128)S(1)}, s32[47]{0:T(128)S(1)}, f32[16,32,256]{2,1,0:T(8,128)S(1)}, bf16[16,2,256,256]{3,2,1,0:T(8,128)(2,1)S(1)}, bf16[16,...) custom-call(s32[4,4,8]{2,1,0:T(4,128)S(1)} %get-tuple-element.31.pair_ref, ...), custom_call_target="tpu_custom_call" | custom-call | flops 201326592 | bytes 557568 | tf_op jit(solution)/shard_map/own_first_kernel/pallas_call | solution.py:373
  11.5 0.0 collective-permute-done.1
  11.5 0.0 collective-permute-done
  11.6 0.1 collective-permute-start.3
  11.7 0.7 %collective-permute-start.2 = (f32[6,34,256]{2,1,0:T(8,128)S(1)}, f32[6,34,256]{2,1,0:T(8,128)S(1)}, u32[]{:S(2)}, u32[]{:S(2)}) collective-permute-start(f32[6,34,256]{2,1,0:T(8,128)S(1)} %get-tuple-element.67), channel_id=1, source_target_pairs={{1,2},{2,1},{3,4},{4,3},{5,6},{6,5},{9,10},{10,9},{11,12},{12,11},... | collective-permute-start | bytes 626696 | tf_op jit(solution)/shard_map/ppermute | solution.py:365
  12.3 2.1 %inner_first_kernel.1 = (f32[16,32,256]{2,1,0:T(8,128)S(1)}, bf16[44,2,256,256]{3,2,1,0:T(8,128)(2,1)S(1)}) custom-call(s32[45]{0:T(128)S(1)} %get-tuple-element.35.items_ref.near_ref, f32[16,32,256]{2,1,0:T(8,128)S(1)} %get-tuple-element.38.sum_ref, bf16[16,64,256]{2,1,0:T(8,128)(2,1)S(1)} %get-tuple-element.39.parts_ref, ...), custom_call_target="tpu_custom_call" | custom-call | flops 528482304 | bytes 5800116 | tf_op jit(solution)/shard_map/inner_first_kernel/pallas_call | solution.py:373
  14.5 0.0 collective-permute-done.3
  14.5 0.0 collective-permute-done.2
  14.5 1.6 %cross_first_kernel.1 = (f32[16,32,256]{2,1,0:T(8,128)S(1)}, bf16[46,2,256,256]{3,2,1,0:T(8,128)(2,1)S(1)}) custom-call(s32[47]{0:T(128)S(1)} %get-tuple-element.34.items_ref.cross_ref, f32[16,32,256]{2,1,0:T(8,128)S(1)} %get-tuple-element.42.sum_ref, f32[4,34,256]{2,1,0:T(8,128)S(1)} %get-tuple-element.43.north_ref, ...), custom_call_target="tpu_custom_call" | custom-call | flops 553648128 | bytes 5415100 | tf_op jit(solution)/shard_map/cross_first_kernel/pallas_call | solution.py:373
  16.2 5.3 %collective-permute-start.5 = (f32[4,32,256]{2,1,0:T(8,128)S(1)}, f32[4,32,256]{2,1,0:T(8,128)S(1)}, u32[]{:S(2)}, u32[]{:S(2)}) collective-permute-start(f32[4,32,256]{2,1,0:T(8,128)S(1)} %get-tuple-element.62), channel_id=1, source_target_pairs={{0,8},{8,0},{16,24},{24,16},{1,9},{9,1},{17,25},{25,17},{2,10},{10... | collective-permute-start | bytes 393224 | tf_op jit(solution)/shard_map/ppermute | solution.py:364
  21.5 0.7 %collective-permute-start.4 = (f32[4,32,256]{2,1,0:T(8,128)S(1)}, f32[4,32,256]{2,1,0:T(8,128)S(1)}, u32[]{:S(2)}, u32[]{:S(2)}) collective-permute-start(f32[4,32,256]{2,1,0:T(8,128)S(1)} %get-tuple-element.63), channel_id=1, source_target_pairs={{8,16},{16,8},{9,17},{17,9},{10,18},{18,10},{11,19},{19,11},{12,20... | collective-permute-start | bytes 393224 | tf_op jit(solution)/shard_map/ppermute | solution.py:365
  22.2 2.2 %near_again_kernel.1 = (f32[16,32,256]{2,1,0:T(8,128)S(1)}, bf16[16,64,256]{2,1,0:T(8,128)(2,1)S(1)}) custom-call(s32[45]{0:T(128)S(1)} %get-tuple-element.35.items_ref.near_ref, f32[16,32,256]{2,1,0:T(8,128)S(1)} %get-tuple-element.47.v_ref.v1_ref, bf16[16,2,256,256]{3,2,1,0:T(8,128)(2,1)S(1)} %get-tuple-element.48.own_ref, ...), custom_call_target="tpu_custom_call" | custom-call | flops 729808896 | bytes 31981748 | tf_op jit(solution)/shard_map/near_again_kernel/pallas_call | solution.py:373
  24.4 0.1 collective-permute-done.5
  24.5 0.0 collective-permute-done.4
  24.6 5.7 %collective-permute-start.7 = (f32[6,32,256]{2,1,0:T(8,128)S(1)}, f32[6,32,256]{2,1,0:T(8,128)S(1)}, u32[]{:S(2)}, u32[]{:S(2)}) collective-permute-start(f32[6,32,256]{2,1,0:T(8,128)S(1)} %get-tuple-element.70), channel_id=1, source_target_pairs={{0,1},{1,0},{2,3},{3,2},{4,5},{5,4},{6,7},{7,6},{8,9},{9,8},{10,11... | collective-permute-start | bytes 589832 | tf_op jit(solution)/shard_map/ppermute | solution.py:364
  30.3 0.7 %collective-permute-start.6 = (f32[6,32,256]{2,1,0:T(8,128)S(1)}, f32[6,32,256]{2,1,0:T(8,128)S(1)}, u32[]{:S(2)}, u32[]{:S(2)}) collective-permute-start(f32[6,32,256]{2,1,0:T(8,128)S(1)} %get-tuple-element.71), channel_id=1, source_target_pairs={{1,2},{2,1},{3,4},{4,3},{5,6},{6,5},{9,10},{10,9},{11,12},{12,11},... | collective-permute-start | bytes 589832 | tf_op jit(solution)/shard_map/ppermute | solution.py:365
  30.9 1.6 %rest_again_kernel.1.sum_ref = f32[16,32,256]{2,1,0:T(8,128)S(1)} custom-call(s32[45]{0:T(128)S(1)} %get-tuple-element.35.items_ref.near_ref, s32[47]{0:T(128)S(1)} %get-tuple-element.34.items_ref.cross_ref, f32[16,32,256]{2,1,0:T(8,128)S(1)} %get-tuple-element.51.sum_ref, bf16[16,64,256]{2,1,0:T(8,128)(2,1)S(1)} %get-tuple-element.52.parts_ref, ...), custom_call_target="tpu_custom_call" | custom-call | flops 528482304 | bytes 49021296 | tf_op jit(solution)/shard_map/rest_again_kernel/pallas_call | solution.py:373
  32.5 0.0 collective-permute-done.7
  32.5 0.0 collective-permute-done.6
  32.6 1.4 %cross_again_kernel.1 = (f32[16,32,256]{2,1,0:T(8,128)S(1)}, f32[32,1,128]{2,1,0:T(1,128)S(1)}) custom-call(s32[47]{0:T(128)S(1)} %get-tuple-element.34.items_ref.cross_ref, f32[16,32,256]{2,1,0:T(8,128)S(1)} %rest_again_kernel.1.sum_ref, f32[6,32,256]{2,1,0:T(8,128)S(1)} %get-tuple-element.69.west_ref, f32[6,32,256]{2,1,0:T(8,128)S(1)} %get-tuple-element.68.east_ref, ...), custom_call_target="tpu_custom_call" | custom-call | flops 553648128 | bytes 26083516 | tf_op jit(solution)/shard_map/cross_again_kernel/pallas_call | solution.py:373
  34.0 25.5 %all_to_all.5.moments_ref = f32[32,1,128]{2,1,0:T(1,128)S(1)} all-to-all(f32[32,1,128]{2,1,0:T(1,128)S(1)} %get-tuple-element.56), channel_id=1, replica_groups=mesh['region'=4,'tile'=8] {'region','tile'}, dimensions={0} | all-to-all | bytes 32768 | tf_op jit(solution)/shard_map/all_to_all | solution.py:458
  59.5 1.3 %final_kernel.1 = (f32[16,32,256]{2,1,0:T(8,128)}, f32[16,32,256]{2,1,0:T(8,128)}) custom-call(f32[32,1,128]{2,1,0:T(1,128)S(1)} %all_to_all.5.moments_ref, f32[16,32,256]{2,1,0:T(8,128)S(1)} %get-tuple-element.32.v_ref.v0_ref, f32[16,32,256]{2,1,0:T(8,128)S(1)} %get-tuple-element.47.v_ref.v1_ref, f32[16,32,256]{2,1,0:T(8,128)S(1)} %get-tuple-element.57.v2_ref), custom_call_target="tpu_custom_call" | custom-call | bytes 1589248 | tf_op jit(solution)/shard_map/final_kernel/pallas_call | solution.py:373
  (12 shorter events, 0.3 us)
Async XLA Ops:
  2.7 8.8 %collective-permute-start.1 = (f32[4,34,256]{2,1,0:T(8,128)S(1)}, f32[4,34,256]{2,1,0:T(8,128)S(1)}, u32[]{:S(2)}, u32[]{:S(2)}) collective-permute-start(f32[4,34,256]{2,1,0:T(8,128)S(1)} %get-tuple-element.74), channel_id=1, source_target_pairs={{0,8},{8,0},{16,24},{24,16},{1,9},{9,1},{17,25},{25,17},{2,10},{10... | collective-permute-start | bytes 417800 | tf_op jit(solution)/shard_map/ppermute | solution.py:364
  5.7 5.8 %collective-permute-start = (f32[4,34,256]{2,1,0:T(8,128)S(1)}, f32[4,34,256]{2,1,0:T(8,128)S(1)}, u32[]{:S(2)}, u32[]{:S(2)}) collective-permute-start(f32[4,34,256]{2,1,0:T(8,128)S(1)} %get-tuple-element.75), channel_id=1, source_target_pairs={{8,16},{16,8},{9,17},{17,9},{10,18},{18,10},{11,19},{19,11},{12,20... | collective-permute-start | bytes 417800 | tf_op jit(solution)/shard_map/ppermute | solution.py:365
  11.6 2.9 %collective-permute-start.3 = (f32[6,34,256]{2,1,0:T(8,128)S(1)}, f32[6,34,256]{2,1,0:T(8,128)S(1)}, u32[]{:S(2)}, u32[]{:S(2)}) collective-permute-start(f32[6,34,256]{2,1,0:T(8,128)S(1)} %get-tuple-element.66), channel_id=1, source_target_pairs={{0,1},{1,0},{2,3},{3,2},{4,5},{5,4},{6,7},{7,6},{8,9},{9,8},{10,11... | collective-permute-start | bytes 626696 | tf_op jit(solution)/shard_map/ppermute | solution.py:364
  11.7 2.8 %collective-permute-start.2 = (f32[6,34,256]{2,1,0:T(8,128)S(1)}, f32[6,34,256]{2,1,0:T(8,128)S(1)}, u32[]{:S(2)}, u32[]{:S(2)}) collective-permute-start(f32[6,34,256]{2,1,0:T(8,128)S(1)} %get-tuple-element.67), channel_id=1, source_target_pairs={{1,2},{2,1},{3,4},{4,3},{5,6},{6,5},{9,10},{10,9},{11,12},{12,11},... | collective-permute-start | bytes 626696 | tf_op jit(solution)/shard_map/ppermute | solution.py:365
  16.2 8.2 %collective-permute-start.5 = (f32[4,32,256]{2,1,0:T(8,128)S(1)}, f32[4,32,256]{2,1,0:T(8,128)S(1)}, u32[]{:S(2)}, u32[]{:S(2)}) collective-permute-start(f32[4,32,256]{2,1,0:T(8,128)S(1)} %get-tuple-element.62), channel_id=1, source_target_pairs={{0,8},{8,0},{16,24},{24,16},{1,9},{9,1},{17,25},{25,17},{2,10},{10... | collective-permute-start | bytes 393224 | tf_op jit(solution)/shard_map/ppermute | solution.py:364
  21.5 3.0 %collective-permute-start.4 = (f32[4,32,256]{2,1,0:T(8,128)S(1)}, f32[4,32,256]{2,1,0:T(8,128)S(1)}, u32[]{:S(2)}, u32[]{:S(2)}) collective-permute-start(f32[4,32,256]{2,1,0:T(8,128)S(1)} %get-tuple-element.63), channel_id=1, source_target_pairs={{8,16},{16,8},{9,17},{17,9},{10,18},{18,10},{11,19},{19,11},{12,20... | collective-permute-start | bytes 393224 | tf_op jit(solution)/shard_map/ppermute | solution.py:365
  24.6 8.0 %collective-permute-start.7 = (f32[6,32,256]{2,1,0:T(8,128)S(1)}, f32[6,32,256]{2,1,0:T(8,128)S(1)}, u32[]{:S(2)}, u32[]{:S(2)}) collective-permute-start(f32[6,32,256]{2,1,0:T(8,128)S(1)} %get-tuple-element.70), channel_id=1, source_target_pairs={{0,1},{1,0},{2,3},{3,2},{4,5},{5,4},{6,7},{7,6},{8,9},{9,8},{10,11... | collective-permute-start | bytes 589832 | tf_op jit(solution)/shard_map/ppermute | solution.py:364
  30.3 2.3 %collective-permute-start.6 = (f32[6,32,256]{2,1,0:T(8,128)S(1)}, f32[6,32,256]{2,1,0:T(8,128)S(1)}, u32[]{:S(2)}, u32[]{:S(2)}) collective-permute-start(f32[6,32,256]{2,1,0:T(8,128)S(1)} %get-tuple-element.71), channel_id=1, source_target_pairs={{1,2},{2,1},{3,4},{4,3},{5,6},{6,5},{9,10},{10,9},{11,12},{12,11},... | collective-permute-start | bytes 589832 | tf_op jit(solution)/shard_map/ppermute | solution.py:365

commit v4 on v3

--- a/solution.py
+++ b/solution.py
@@ -91,7 +91,7 @@
 
 
 def only_use(first, last, kept_ref, use):
-    in_turns(first, last, lambda n: use(kept_ref[n, 0], kept_ref[n, 1], n))
+    in_turns(first, last, lambda n: use(kept_ref[n, 0], kept_ref[n, 1], n), (4, 3, 2, 1, 0))
 
 
 def item_code(own, other, shift_a, shift_b):
@@ -300,7 +300,8 @@
 
 
 def rest_again_kernel(
-    near_ref, cross_ref, sum_ref, parts_ref, near_kept_ref, north_ref, south_ref, cross_kept_ref, out_ref, round_ref
+    near_ref, cross_ref, sum_ref, parts_ref, near_kept_ref, north_ref, south_ref, cross_kept_ref, v0_ref, v1_ref,
+    out_ref, terms_ref, round_ref
 ):
     out_ref[...] = sum_ref[...]
     use = functools.partial(use_pair, out_ref, parts_ref, near_ref)
@@ -309,9 +310,17 @@
     in_rows = cross_ref[cross_ref.shape[0] - 1]
     only_use(0, in_rows, cross_kept_ref, functools.partial(use_cross, out_ref, round_ref, cross_ref))
 
+    def gather(at, sums):
+        w0, w1 = v0_ref[at], v1_ref[at]
+        return tuple(s + t for s, t in zip(sums, (w0 * w0, w0 * w1, w1 * w1)))
+
+    zero = jnp.zeros(out_ref.shape[1:], jnp.float32)
+    for n, total in enumerate(lax.fori_loop(0, out_ref.shape[0], gather, (zero,) * 3)):
+        terms_ref[n] = total
+
 
 def cross_again_kernel(
-    items_ref, sum_ref, west_ref, east_ref, kept_ref, v0_ref, v1_ref, out_ref, moments_ref, parts_ref
+    items_ref, sum_ref, west_ref, east_ref, kept_ref, terms_ref, v1_ref, out_ref, moments_ref, parts_ref
 ):
     out_ref[...] = sum_ref[...]
     start = parts_ref.shape[0] - west_ref.shape[0] - east_ref.shape[0]
@@ -319,13 +328,8 @@
     in_rows = items_ref[items_ref.shape[0] - 1]
     only_use(in_rows, items_ref[0], kept_ref, functools.partial(use_cross, out_ref, parts_ref, items_ref))
     zero = jnp.zeros(out_ref.shape[1:], jnp.float32)
-
-    def gather(at, sums):
-        w0, w1, w2 = v0_ref[at], v1_ref[at], out_ref[at]
-        terms = (w0 * w0, w0 * w1, w1 * w1, w1 * w2)
-        return tuple(s + t for s, t in zip(sums, terms))
-
-    sums = lax.fori_loop(0, out_ref.shape[0], gather, (zero,) * 4)
+    last = lax.fori_loop(0, out_ref.shape[0], lambda at, total: total + v1_ref[at] * out_ref[at], zero)
+    sums = [terms_ref[n] for n in range(3)] + [last]
     lanes = moments_ref.shape[2]
     folded = [sum(s[:, left : left + lanes] for left in range(0, s.shape[1], lanes)) for s in sums]
     stacked = jnp.concatenate(folded, axis=0)
@@ -446,14 +450,14 @@
     )
     north, south, part = lax.optimization_barrier((north, south, part))
     west, east = columns_round(w1_grid[:, 0], w1_grid[:, cols - 1], north, south)
-    (part,) = on_device(
-        rest_again_kernel, (field,),
-        (near_items, cross_items, part, parts, near_tiles, north, south, cross_tiles), (parts_round,), True,
+    part, terms = on_device(
+        rest_again_kernel, (field, array((3, rhs, points), f32)),
+        (near_items, cross_items, part, parts, near_tiles, north, south, cross_tiles, w0, w1), (parts_round,), True,
         near_count * each,
     )
     w2, moments = on_device(
         cross_again_kernel, (field, array((devices, 1, 4 * rhs), f32)),
-        (cross_items, part, west, east, cross_tiles, w0, w1), (parts_round,), True, cross_count * each,
+        (cross_items, part, west, east, cross_tiles, terms, w1), (parts_round,), True, cross_count * each,
     )
     moments = lax.all_to_all(moments, ("region", "tile"), 0, 0)
     solution, residual = on_device(final_kernel, (field, field), (moments, w0, w1, w2))

time: 61.8 us -> 63.3 us (1.024); the launches traced: 60.8 us -> 64.5 us
  Pallas kernels: 17.3 us -> 20.3 us
  blocking collectives: 25.5 us -> 27.8 us
  starting transfers between devices: 16.8 us -> 15.2 us
    pallas_call x8, Pallas kernels: 17.3 us -> 20.3 us  [on_device(): pl.pallas_call(kernel, out_shape=tuple(outputs), in_specs=[smem if listed...]
    all_to_all x1, blocking collectives: 25.5 us -> 27.8 us  [per_device(): moments = lax.all_to_all(moments, ('region', 'tile'), 0, 0)]
    ppermute x4, starting transfers between devices: 14.1 us -> 12.6 us  [swapped(): got_up = lax.ppermute(jnp.where(even, last, first), axis, swap_up)]
  transfers between devices with their start and end apart: 8 -> 8, of which waited for: 1 -> 0; matrix products, arithmetic and copies ran while one was open for 0% -> 0% of each run, Pallas kernels for 18% -> 22%
where the time goes in v4:
time: 63.3 us; the launch traced here: 64.5 us
  blocking collectives  27.8 us (44%)
  Pallas kernels  20.3 us (32%)
  starting transfers between devices  15.2 us (24%)
  between operations  0.9 us (1%)
    all_to_all x1, blocking collectives, per_device(): moments = lax.all_to_all(moments, ('region', 'tile'), 0, 0)  27.8 us
    pallas_call x8, Pallas kernels, on_device(): pl.pallas_call(kernel, out_shape=tuple(outputs), in_specs=[smem if listed...  20.3 us
    ppermute x4, starting transfers between devices, swapped(): got_up = lax.ppermute(jnp.where(even, last, first), axis, swap_up)  12.6 us
    ppermute x4, starting transfers between devices, swapped(): got_down = lax.ppermute(jnp.where(even, first, last), axis, swap_down)  2.65 us
  transfers between devices with their start and end apart: 8, of which 0 were waited for; matrix products, arithmetic and copies ran while one was open for 0% of the time, Pallas kernels for 22%

profile of v4, /device:TPU:0, one launch (start us, length us, event | category | flops | bytes accessed | tf_op | source)
XLA Modules:
  0.0 64.5 jit_solution(17369995238500555175)
XLA Ops:
  0.6 2.0 %pack_kernel.1 = (f32[4,34,256]{2,1,0:T(8,128)S(1)}, f32[4,34,256]{2,1,0:T(8,128)S(1)}, f32[2,4,34,256]{3,2,1,0:T(8,128)S(1)}, f32[16,32,256]{2,1,0:T(8,128)S(1)...) custom-call(f32[4,4,32,256]{3,2,1,0:T(8,128)} %v_hbm.1, f32[4,4,2,256]{3,2,1,0:T(2,128)} %c_hbm.1, s32[4,4,8]{2,1,0:T(4,128)} %bitcast.17), custom_call_target="tpu_custom_call" | custom-call | bytes 557568 | tf_op jit(solution)/shard_map/pack_kernel/pallas_call | solution.py:377
  2.7 3.0 %collective-permute-start.1 = (f32[4,34,256]{2,1,0:T(8,128)S(1)}, f32[4,34,256]{2,1,0:T(8,128)S(1)}, u32[]{:S(2)}, u32[]{:S(2)}) collective-permute-start(f32[4,34,256]{2,1,0:T(8,128)S(1)} %get-tuple-element.78), channel_id=1, source_target_pairs={{0,8},{8,0},{16,24},{24,16},{1,9},{9,1},{17,25},{25,17},{2,10},{10... | collective-permute-start | bytes 417800 | tf_op jit(solution)/shard_map/ppermute | solution.py:368
  5.7 0.7 %collective-permute-start = (f32[4,34,256]{2,1,0:T(8,128)S(1)}, f32[4,34,256]{2,1,0:T(8,128)S(1)}, u32[]{:S(2)}, u32[]{:S(2)}) collective-permute-start(f32[4,34,256]{2,1,0:T(8,128)S(1)} %get-tuple-element.79), channel_id=1, source_target_pairs={{8,16},{16,8},{9,17},{17,9},{10,18},{18,10},{11,19},{19,11},{12,20... | collective-permute-start | bytes 417800 | tf_op jit(solution)/shard_map/ppermute | solution.py:369
  6.4 5.1 %own_first_kernel.1 = (s32[45]{0:T(128)S(1)}, s32[47]{0:T(128)S(1)}, f32[16,32,256]{2,1,0:T(8,128)S(1)}, bf16[16,2,256,256]{3,2,1,0:T(8,128)(2,1)S(1)}, bf16[16,...) custom-call(s32[4,4,8]{2,1,0:T(4,128)S(1)} %get-tuple-element.33.pair_ref, ...), custom_call_target="tpu_custom_call" | custom-call | flops 201326592 | bytes 557568 | tf_op jit(solution)/shard_map/own_first_kernel/pallas_call | solution.py:377
  11.5 0.0 collective-permute-done.1
  11.5 0.0 collective-permute-done
  11.6 0.1 collective-permute-start.3
  11.7 0.7 %collective-permute-start.2 = (f32[6,34,256]{2,1,0:T(8,128)S(1)}, f32[6,34,256]{2,1,0:T(8,128)S(1)}, u32[]{:S(2)}, u32[]{:S(2)}) collective-permute-start(f32[6,34,256]{2,1,0:T(8,128)S(1)} %get-tuple-element.71), channel_id=1, source_target_pairs={{1,2},{2,1},{3,4},{4,3},{5,6},{6,5},{9,10},{10,9},{11,12},{12,11},... | collective-permute-start | bytes 626696 | tf_op jit(solution)/shard_map/ppermute | solution.py:369
  12.4 3.9 %inner_first_kernel.1 = (f32[16,32,256]{2,1,0:T(8,128)S(1)}, bf16[44,2,256,256]{3,2,1,0:T(8,128)(2,1)S(1)}) custom-call(s32[45]{0:T(128)S(1)} %get-tuple-element.37.items_ref.near_ref, f32[16,32,256]{2,1,0:T(8,128)S(1)} %get-tuple-element.40.sum_ref, bf16[16,64,256]{2,1,0:T(8,128)(2,1)S(1)} %get-tuple-element.41.parts_ref, ...), custom_call_target="tpu_custom_call" | custom-call | flops 528482304 | bytes 5800116 | tf_op jit(solution)/shard_map/inner_first_kernel/pallas_call | solution.py:377
  16.3 0.0 collective-permute-done.3
  16.3 0.0 collective-permute-done.2
  16.4 1.7 %cross_first_kernel.1 = (f32[16,32,256]{2,1,0:T(8,128)S(1)}, bf16[46,2,256,256]{3,2,1,0:T(8,128)(2,1)S(1)}) custom-call(s32[47]{0:T(128)S(1)} %get-tuple-element.36.items_ref.cross_ref, f32[16,32,256]{2,1,0:T(8,128)S(1)} %get-tuple-element.44.sum_ref, f32[4,34,256]{2,1,0:T(8,128)S(1)} %get-tuple-element.45.north_ref, ...), custom_call_target="tpu_custom_call" | custom-call | flops 553648128 | bytes 5415100 | tf_op jit(solution)/shard_map/cross_first_kernel/pallas_call | solution.py:377
  18.1 3.2 %collective-permute-start.5 = (f32[4,32,256]{2,1,0:T(8,128)S(1)}, f32[4,32,256]{2,1,0:T(8,128)S(1)}, u32[]{:S(2)}, u32[]{:S(2)}) collective-permute-start(f32[4,32,256]{2,1,0:T(8,128)S(1)} %get-tuple-element.66), channel_id=1, source_target_pairs={{0,8},{8,0},{16,24},{24,16},{1,9},{9,1},{17,25},{25,17},{2,10},{10... | collective-permute-start | bytes 393224 | tf_op jit(solution)/shard_map/ppermute | solution.py:368
  21.3 0.7 %collective-permute-start.4 = (f32[4,32,256]{2,1,0:T(8,128)S(1)}, f32[4,32,256]{2,1,0:T(8,128)S(1)}, u32[]{:S(2)}, u32[]{:S(2)}) collective-permute-start(f32[4,32,256]{2,1,0:T(8,128)S(1)} %get-tuple-element.67), channel_id=1, source_target_pairs={{8,16},{16,8},{9,17},{17,9},{10,18},{18,10},{11,19},{19,11},{12,20... | collective-permute-start | bytes 393224 | tf_op jit(solution)/shard_map/ppermute | solution.py:369
  22.0 2.7 %near_again_kernel.1 = (f32[16,32,256]{2,1,0:T(8,128)S(1)}, bf16[16,64,256]{2,1,0:T(8,128)(2,1)S(1)}) custom-call(s32[45]{0:T(128)S(1)} %get-tuple-element.37.items_ref.near_ref, f32[16,32,256]{2,1,0:T(8,128)S(1)} %get-tuple-element.49.v_ref.v1_ref, bf16[16,2,256,256]{3,2,1,0:T(8,128)(2,1)S(1)} %get-tuple-element.50.own_ref, ...), custom_call_target="tpu_custom_call" | custom-call | flops 729808896 | bytes 31981748 | tf_op jit(solution)/shard_map/near_again_kernel/pallas_call | solution.py:377
  24.7 0.0 collective-permute-done.5
  24.7 0.0 collective-permute-done.4
  24.8 6.3 %collective-permute-start.7 = (f32[6,32,256]{2,1,0:T(8,128)S(1)}, f32[6,32,256]{2,1,0:T(8,128)S(1)}, u32[]{:S(2)}, u32[]{:S(2)}) collective-permute-start(f32[6,32,256]{2,1,0:T(8,128)S(1)} %get-tuple-element.74), channel_id=1, source_target_pairs={{0,1},{1,0},{2,3},{3,2},{4,5},{5,4},{6,7},{7,6},{8,9},{9,8},{10,11... | collective-permute-start | bytes 589832 | tf_op jit(solution)/shard_map/ppermute | solution.py:368
  31.1 0.7 %collective-permute-start.6 = (f32[6,32,256]{2,1,0:T(8,128)S(1)}, f32[6,32,256]{2,1,0:T(8,128)S(1)}, u32[]{:S(2)}, u32[]{:S(2)}) collective-permute-start(f32[6,32,256]{2,1,0:T(8,128)S(1)} %get-tuple-element.75), channel_id=1, source_target_pairs={{1,2},{2,1},{3,4},{4,3},{5,6},{6,5},{9,10},{10,9},{11,12},{12,11},... | collective-permute-start | bytes 589832 | tf_op jit(solution)/shard_map/ppermute | solution.py:369
  31.8 2.4 %rest_again_kernel.1 = (f32[16,32,256]{2,1,0:T(8,128)S(1)}, f32[3,32,256]{2,1,0:T(8,128)S(1)}) custom-call(s32[45]{0:T(128)S(1)} %get-tuple-element.37.items_ref.near_ref, s32[47]{0:T(128)S(1)} %get-tuple-element.36.items_ref.cross_ref, f32[16,32,256]{2,1,0:T(8,128)S(1)} %get-tuple-element.53.sum_ref, bf16[16,64,256]{2,1,0:T(8,128)(2,1)S(1)} %get-tuple-element.54.parts_ref, ...), custom_call_target="tpu_custom_call" | custom-call | flops 528482304 | bytes 50069872 | tf_op jit(solution)/shard_map/rest_again_kernel/pallas_call | solution.py:377
  34.2 0.0 collective-permute-done.7
  34.2 0.0 collective-permute-done.6
  34.2 1.2 %cross_again_kernel.1 = (f32[16,32,256]{2,1,0:T(8,128)S(1)}, f32[32,1,128]{2,1,0:T(1,128)S(1)}) custom-call(s32[47]{0:T(128)S(1)} %get-tuple-element.36.items_ref.cross_ref, f32[16,32,256]{2,1,0:T(8,128)S(1)} %get-tuple-element.58.sum_ref, f32[6,32,256]{2,1,0:T(8,128)S(1)} %get-tuple-element.73.west_ref, f32[6,32,256]{2,1,0:T(8,128)S(1)} %get-tuple-element.72.east_ref, ...), custom_call_target="tpu_custom_call" | custom-call | flops 553648128 | bytes 25657532 | tf_op jit(solution)/shard_map/cross_again_kernel/pallas_call | solution.py:377
  35.4 27.8 %all_to_all.5.moments_ref = f32[32,1,128]{2,1,0:T(1,128)S(1)} all-to-all(f32[32,1,128]{2,1,0:T(1,128)S(1)} %get-tuple-element.60), channel_id=1, replica_groups=mesh['region'=4,'tile'=8] {'region','tile'}, dimensions={0} | all-to-all | bytes 32768 | tf_op jit(solution)/shard_map/all_to_all | solution.py:462
  63.2 1.3 %final_kernel.1 = (f32[16,32,256]{2,1,0:T(8,128)}, f32[16,32,256]{2,1,0:T(8,128)}) custom-call(f32[32,1,128]{2,1,0:T(1,128)S(1)} %all_to_all.5.moments_ref, f32[16,32,256]{2,1,0:T(8,128)S(1)} %get-tuple-element.34.v_ref.v0_ref, f32[16,32,256]{2,1,0:T(8,128)S(1)} %get-tuple-element.49.v_ref.v1_ref, f32[16,32,256]{2,1,0:T(8,128)S(1)} %get-tuple-element.61.v2_ref), custom_call_target="tpu_custom_call" | custom-call | bytes 1589248 | tf_op jit(solution)/shard_map/final_kernel/pallas_call | solution.py:377
  (12 shorter events, 0.3 us)
Async XLA Ops:
  2.7 8.8 %collective-permute-start.1 = (f32[4,34,256]{2,1,0:T(8,128)S(1)}, f32[4,34,256]{2,1,0:T(8,128)S(1)}, u32[]{:S(2)}, u32[]{:S(2)}) collective-permute-start(f32[4,34,256]{2,1,0:T(8,128)S(1)} %get-tuple-element.78), channel_id=1, source_target_pairs={{0,8},{8,0},{16,24},{24,16},{1,9},{9,1},{17,25},{25,17},{2,10},{10... | collective-permute-start | bytes 417800 | tf_op jit(solution)/shard_map/ppermute | solution.py:368
  5.7 5.8 %collective-permute-start = (f32[4,34,256]{2,1,0:T(8,128)S(1)}, f32[4,34,256]{2,1,0:T(8,128)S(1)}, u32[]{:S(2)}, u32[]{:S(2)}) collective-permute-start(f32[4,34,256]{2,1,0:T(8,128)S(1)} %get-tuple-element.79), channel_id=1, source_target_pairs={{8,16},{16,8},{9,17},{17,9},{10,18},{18,10},{11,19},{19,11},{12,20... | collective-permute-start | bytes 417800 | tf_op jit(solution)/shard_map/ppermute | solution.py:369
  11.6 4.7 %collective-permute-start.3 = (f32[6,34,256]{2,1,0:T(8,128)S(1)}, f32[6,34,256]{2,1,0:T(8,128)S(1)}, u32[]{:S(2)}, u32[]{:S(2)}) collective-permute-start(f32[6,34,256]{2,1,0:T(8,128)S(1)} %get-tuple-element.70), channel_id=1, source_target_pairs={{0,1},{1,0},{2,3},{3,2},{4,5},{5,4},{6,7},{7,6},{8,9},{9,8},{10,11... | collective-permute-start | bytes 626696 | tf_op jit(solution)/shard_map/ppermute | solution.py:368
  11.7 4.6 %collective-permute-start.2 = (f32[6,34,256]{2,1,0:T(8,128)S(1)}, f32[6,34,256]{2,1,0:T(8,128)S(1)}, u32[]{:S(2)}, u32[]{:S(2)}) collective-permute-start(f32[6,34,256]{2,1,0:T(8,128)S(1)} %get-tuple-element.71), channel_id=1, source_target_pairs={{1,2},{2,1},{3,4},{4,3},{5,6},{6,5},{9,10},{10,9},{11,12},{12,11},... | collective-permute-start | bytes 626696 | tf_op jit(solution)/shard_map/ppermute | solution.py:369
  18.1 6.6 %collective-permute-start.5 = (f32[4,32,256]{2,1,0:T(8,128)S(1)}, f32[4,32,256]{2,1,0:T(8,128)S(1)}, u32[]{:S(2)}, u32[]{:S(2)}) collective-permute-start(f32[4,32,256]{2,1,0:T(8,128)S(1)} %get-tuple-element.66), channel_id=1, source_target_pairs={{0,8},{8,0},{16,24},{24,16},{1,9},{9,1},{17,25},{25,17},{2,10},{10... | collective-permute-start | bytes 393224 | tf_op jit(solution)/shard_map/ppermute | solution.py:368
  21.3 3.4 %collective-permute-start.4 = (f32[4,32,256]{2,1,0:T(8,128)S(1)}, f32[4,32,256]{2,1,0:T(8,128)S(1)}, u32[]{:S(2)}, u32[]{:S(2)}) collective-permute-start(f32[4,32,256]{2,1,0:T(8,128)S(1)} %get-tuple-element.67), channel_id=1, source_target_pairs={{8,16},{16,8},{9,17},{17,9},{10,18},{18,10},{11,19},{19,11},{12,20... | collective-permute-start | bytes 393224 | tf_op jit(solution)/shard_map/ppermute | solution.py:369
  24.8 9.3 %collective-permute-start.7 = (f32[6,32,256]{2,1,0:T(8,128)S(1)}, f32[6,32,256]{2,1,0:T(8,128)S(1)}, u32[]{:S(2)}, u32[]{:S(2)}) collective-permute-start(f32[6,32,256]{2,1,0:T(8,128)S(1)} %get-tuple-element.74), channel_id=1, source_target_pairs={{0,1},{1,0},{2,3},{3,2},{4,5},{5,4},{6,7},{7,6},{8,9},{9,8},{10,11... | collective-permute-start | bytes 589832 | tf_op jit(solution)/shard_map/ppermute | solution.py:368
  31.1 3.0 %collective-permute-start.6 = (f32[6,32,256]{2,1,0:T(8,128)S(1)}, f32[6,32,256]{2,1,0:T(8,128)S(1)}, u32[]{:S(2)}, u32[]{:S(2)}) collective-permute-start(f32[6,32,256]{2,1,0:T(8,128)S(1)} %get-tuple-element.75), channel_id=1, source_target_pairs={{1,2},{2,1},{3,4},{4,3},{5,6},{6,5},{9,10},{10,9},{11,12},{12,11},... | collective-permute-start | bytes 589832 | tf_op jit(solution)/shard_map/ppermute | solution.py:369

commit v5 on v4

--- a/solution.py
+++ b/solution.py
@@ -244,7 +244,7 @@
         )
         out_ref[own] += total[0]
 
-    in_turns(0, items_ref[0], make)
+    in_turns(0, items_ref[0], make, (4, 3, 2, 1, 0))
 
 
 def take_round(round_refs, rhs, parts_ref, points_ref=None, start=0):

time: 63.3 us -> 65 us (1.027); the launches traced: 64.5 us -> 65 us
  Pallas kernels: 20.3 us -> 17.1 us
  blocking collectives: 27.8 us -> 29.9 us
  starting transfers between devices: 15.2 us -> 16.8 us
    pallas_call x8, Pallas kernels: 20.3 us -> 17.1 us  [on_device(): pl.pallas_call(kernel, out_shape=tuple(outputs), in_specs=[smem if listed...]
    all_to_all x1, blocking collectives: 27.8 us -> 29.9 us  [per_device(): moments = lax.all_to_all(moments, ('region', 'tile'), 0, 0)]
    ppermute x4, starting transfers between devices: 12.6 us -> 14.2 us  [swapped(): got_up = lax.ppermute(jnp.where(even, last, first), axis, swap_up)]
  transfers between devices with their start and end apart: 8 -> 8, of which waited for: 0 -> 0; matrix products, arithmetic and copies ran while one was open for 0% -> 0% of each run, Pallas kernels for 22% -> 18%
where the time goes in v5:
time: 65 us
  blocking collectives  29.9 us (46%)
  Pallas kernels  17.1 us (26%)
  starting transfers between devices  16.8 us (26%)
  between operations  0.89 us (1%)
    all_to_all x1, blocking collectives, per_device(): moments = lax.all_to_all(moments, ('region', 'tile'), 0, 0)  29.9 us
    pallas_call x8, Pallas kernels, on_device(): pl.pallas_call(kernel, out_shape=tuple(outputs), in_specs=[smem if listed...  17.1 us
    ppermute x4, starting transfers between devices, swapped(): got_up = lax.ppermute(jnp.where(even, last, first), axis, swap_up)  14.2 us
    ppermute x4, starting transfers between devices, swapped(): got_down = lax.ppermute(jnp.where(even, first, last), axis, swap_down)  2.65 us
  transfers between devices with their start and end apart: 8, of which 0 were waited for; matrix products, arithmetic and copies ran while one was open for 0% of the time, Pallas kernels for 18%

profile of v5, /device:TPU:0, one launch (start us, length us, event | category | flops | bytes accessed | tf_op | source)
XLA Modules:
  0.0 65.0 jit_solution(1178673291045911896)
XLA Ops:
  0.6 2.0 %pack_kernel.1 = (f32[4,34,256]{2,1,0:T(8,128)S(1)}, f32[4,34,256]{2,1,0:T(8,128)S(1)}, f32[2,4,34,256]{3,2,1,0:T(8,128)S(1)}, f32[16,32,256]{2,1,0:T(8,128)S(1)...) custom-call(f32[4,4,32,256]{3,2,1,0:T(8,128)} %v_hbm.1, f32[4,4,2,256]{3,2,1,0:T(2,128)} %c_hbm.1, s32[4,4,8]{2,1,0:T(4,128)} %bitcast.17), custom_call_target="tpu_custom_call" | custom-call | bytes 557568 | tf_op jit(solution)/shard_map/pack_kernel/pallas_call | solution.py:377
  2.7 3.0 %collective-permute-start.1 = (f32[4,34,256]{2,1,0:T(8,128)S(1)}, f32[4,34,256]{2,1,0:T(8,128)S(1)}, u32[]{:S(2)}, u32[]{:S(2)}) collective-permute-start(f32[4,34,256]{2,1,0:T(8,128)S(1)} %get-tuple-element.78), channel_id=1, source_target_pairs={{0,8},{8,0},{16,24},{24,16},{1,9},{9,1},{17,25},{25,17},{2,10},{10... | collective-permute-start | bytes 417800 | tf_op jit(solution)/shard_map/ppermute | solution.py:368
  5.7 0.7 %collective-permute-start = (f32[4,34,256]{2,1,0:T(8,128)S(1)}, f32[4,34,256]{2,1,0:T(8,128)S(1)}, u32[]{:S(2)}, u32[]{:S(2)}) collective-permute-start(f32[4,34,256]{2,1,0:T(8,128)S(1)} %get-tuple-element.79), channel_id=1, source_target_pairs={{8,16},{16,8},{9,17},{17,9},{10,18},{18,10},{11,19},{19,11},{12,20... | collective-permute-start | bytes 417800 | tf_op jit(solution)/shard_map/ppermute | solution.py:369
  6.4 5.1 %own_first_kernel.1 = (s32[45]{0:T(128)S(1)}, s32[47]{0:T(128)S(1)}, f32[16,32,256]{2,1,0:T(8,128)S(1)}, bf16[16,2,256,256]{3,2,1,0:T(8,128)(2,1)S(1)}, bf16[16,...) custom-call(s32[4,4,8]{2,1,0:T(4,128)S(1)} %get-tuple-element.33.pair_ref, ...), custom_call_target="tpu_custom_call" | custom-call | flops 201326592 | bytes 557568 | tf_op jit(solution)/shard_map/own_first_kernel/pallas_call | solution.py:377
  11.5 0.0 collective-permute-done.1
  11.5 0.0 collective-permute-done
  11.6 0.1 collective-permute-start.3
  11.7 0.7 %collective-permute-start.2 = (f32[6,34,256]{2,1,0:T(8,128)S(1)}, f32[6,34,256]{2,1,0:T(8,128)S(1)}, u32[]{:S(2)}, u32[]{:S(2)}) collective-permute-start(f32[6,34,256]{2,1,0:T(8,128)S(1)} %get-tuple-element.71), channel_id=1, source_target_pairs={{1,2},{2,1},{3,4},{4,3},{5,6},{6,5},{9,10},{10,9},{11,12},{12,11},... | collective-permute-start | bytes 626696 | tf_op jit(solution)/shard_map/ppermute | solution.py:369
  12.4 2.4 %inner_first_kernel.1 = (f32[16,32,256]{2,1,0:T(8,128)S(1)}, bf16[44,2,256,256]{3,2,1,0:T(8,128)(2,1)S(1)}) custom-call(s32[45]{0:T(128)S(1)} %get-tuple-element.37.items_ref.near_ref, f32[16,32,256]{2,1,0:T(8,128)S(1)} %get-tuple-element.40.sum_ref, bf16[16,64,256]{2,1,0:T(8,128)(2,1)S(1)} %get-tuple-element.41.parts_ref, ...), custom_call_target="tpu_custom_call" | custom-call | flops 528482304 | bytes 5800116 | tf_op jit(solution)/shard_map/inner_first_kernel/pallas_call | solution.py:377
  14.8 0.0 collective-permute-done.3
  14.8 0.0 collective-permute-done.2
  14.8 1.3 %cross_first_kernel.1 = (f32[16,32,256]{2,1,0:T(8,128)S(1)}, bf16[46,2,256,256]{3,2,1,0:T(8,128)(2,1)S(1)}) custom-call(s32[47]{0:T(128)S(1)} %get-tuple-element.36.items_ref.cross_ref, f32[16,32,256]{2,1,0:T(8,128)S(1)} %get-tuple-element.44.sum_ref, f32[4,34,256]{2,1,0:T(8,128)S(1)} %get-tuple-element.45.north_ref, ...), custom_call_target="tpu_custom_call" | custom-call | flops 553648128 | bytes 5415100 | tf_op jit(solution)/shard_map/cross_first_kernel/pallas_call | solution.py:377
  16.2 6.2 %collective-permute-start.5 = (f32[4,32,256]{2,1,0:T(8,128)S(1)}, f32[4,32,256]{2,1,0:T(8,128)S(1)}, u32[]{:S(2)}, u32[]{:S(2)}) collective-permute-start(f32[4,32,256]{2,1,0:T(8,128)S(1)} %get-tuple-element.66), channel_id=1, source_target_pairs={{0,8},{8,0},{16,24},{24,16},{1,9},{9,1},{17,25},{25,17},{2,10},{10... | collective-permute-start | bytes 393224 | tf_op jit(solution)/shard_map/ppermute | solution.py:368
  22.4 0.7 %collective-permute-start.4 = (f32[4,32,256]{2,1,0:T(8,128)S(1)}, f32[4,32,256]{2,1,0:T(8,128)S(1)}, u32[]{:S(2)}, u32[]{:S(2)}) collective-permute-start(f32[4,32,256]{2,1,0:T(8,128)S(1)} %get-tuple-element.67), channel_id=1, source_target_pairs={{8,16},{16,8},{9,17},{17,9},{10,18},{18,10},{11,19},{19,11},{12,20... | collective-permute-start | bytes 393224 | tf_op jit(solution)/shard_map/ppermute | solution.py:369
  23.0 2.3 %near_again_kernel.1 = (f32[16,32,256]{2,1,0:T(8,128)S(1)}, bf16[16,64,256]{2,1,0:T(8,128)(2,1)S(1)}) custom-call(s32[45]{0:T(128)S(1)} %get-tuple-element.37.items_ref.near_ref, f32[16,32,256]{2,1,0:T(8,128)S(1)} %get-tuple-element.49.v_ref.v1_ref, bf16[16,2,256,256]{3,2,1,0:T(8,128)(2,1)S(1)} %get-tuple-element.50.own_ref, ...), custom_call_target="tpu_custom_call" | custom-call | flops 729808896 | bytes 31981748 | tf_op jit(solution)/shard_map/near_again_kernel/pallas_call | solution.py:377
  25.4 0.0 collective-permute-done.5
  25.4 0.0 collective-permute-done.4
  25.5 4.9 %collective-permute-start.7 = (f32[6,32,256]{2,1,0:T(8,128)S(1)}, f32[6,32,256]{2,1,0:T(8,128)S(1)}, u32[]{:S(2)}, u32[]{:S(2)}) collective-permute-start(f32[6,32,256]{2,1,0:T(8,128)S(1)} %get-tuple-element.74), channel_id=1, source_target_pairs={{0,1},{1,0},{2,3},{3,2},{4,5},{5,4},{6,7},{7,6},{8,9},{9,8},{10,11... | collective-permute-start | bytes 589832 | tf_op jit(solution)/shard_map/ppermute | solution.py:368
  30.4 0.7 %collective-permute-start.6 = (f32[6,32,256]{2,1,0:T(8,128)S(1)}, f32[6,32,256]{2,1,0:T(8,128)S(1)}, u32[]{:S(2)}, u32[]{:S(2)}) collective-permute-start(f32[6,32,256]{2,1,0:T(8,128)S(1)} %get-tuple-element.75), channel_id=1, source_target_pairs={{1,2},{2,1},{3,4},{4,3},{5,6},{6,5},{9,10},{10,9},{11,12},{12,11},... | collective-permute-start | bytes 589832 | tf_op jit(solution)/shard_map/ppermute | solution.py:369
  31.0 1.8 %rest_again_kernel.1 = (f32[16,32,256]{2,1,0:T(8,128)S(1)}, f32[3,32,256]{2,1,0:T(8,128)S(1)}) custom-call(s32[45]{0:T(128)S(1)} %get-tuple-element.37.items_ref.near_ref, s32[47]{0:T(128)S(1)} %get-tuple-element.36.items_ref.cross_ref, f32[16,32,256]{2,1,0:T(8,128)S(1)} %get-tuple-element.53.sum_ref, bf16[16,64,256]{2,1,0:T(8,128)(2,1)S(1)} %get-tuple-element.54.parts_ref, ...), custom_call_target="tpu_custom_call" | custom-call | flops 528482304 | bytes 50069872 | tf_op jit(solution)/shard_map/rest_again_kernel/pallas_call | solution.py:377
  32.8 0.0 collective-permute-done.7
  32.8 0.0 collective-permute-done.6
  32.9 1.0 %cross_again_kernel.1 = (f32[16,32,256]{2,1,0:T(8,128)S(1)}, f32[32,1,128]{2,1,0:T(1,128)S(1)}) custom-call(s32[47]{0:T(128)S(1)} %get-tuple-element.36.items_ref.cross_ref, f32[16,32,256]{2,1,0:T(8,128)S(1)} %get-tuple-element.58.sum_ref, f32[6,32,256]{2,1,0:T(8,128)S(1)} %get-tuple-element.73.west_ref, f32[6,32,256]{2,1,0:T(8,128)S(1)} %get-tuple-element.72.east_ref, ...), custom_call_target="tpu_custom_call" | custom-call | flops 553648128 | bytes 25657532 | tf_op jit(solution)/shard_map/cross_again_kernel/pallas_call | solution.py:377
  33.8 29.9 %all_to_all.5.moments_ref = f32[32,1,128]{2,1,0:T(1,128)S(1)} all-to-all(f32[32,1,128]{2,1,0:T(1,128)S(1)} %get-tuple-element.60), channel_id=1, replica_groups=mesh['region'=4,'tile'=8] {'region','tile'}, dimensions={0} | all-to-all | bytes 32768 | tf_op jit(solution)/shard_map/all_to_all | solution.py:462
  63.7 1.3 %final_kernel.1 = (f32[16,32,256]{2,1,0:T(8,128)}, f32[16,32,256]{2,1,0:T(8,128)}) custom-call(f32[32,1,128]{2,1,0:T(1,128)S(1)} %all_to_all.5.moments_ref, f32[16,32,256]{2,1,0:T(8,128)S(1)} %get-tuple-element.34.v_ref.v0_ref, f32[16,32,256]{2,1,0:T(8,128)S(1)} %get-tuple-element.49.v_ref.v1_ref, f32[16,32,256]{2,1,0:T(8,128)S(1)} %get-tuple-element.61.v2_ref), custom_call_target="tpu_custom_call" | custom-call | bytes 1589248 | tf_op jit(solution)/shard_map/final_kernel/pallas_call | solution.py:377
  (12 shorter events, 0.3 us)
Async XLA Ops:
  2.7 8.8 %collective-permute-start.1 = (f32[4,34,256]{2,1,0:T(8,128)S(1)}, f32[4,34,256]{2,1,0:T(8,128)S(1)}, u32[]{:S(2)}, u32[]{:S(2)}) collective-permute-start(f32[4,34,256]{2,1,0:T(8,128)S(1)} %get-tuple-element.78), channel_id=1, source_target_pairs={{0,8},{8,0},{16,24},{24,16},{1,9},{9,1},{17,25},{25,17},{2,10},{10... | collective-permute-start | bytes 417800 | tf_op jit(solution)/shard_map/ppermute | solution.py:368
  5.7 5.8 %collective-permute-start = (f32[4,34,256]{2,1,0:T(8,128)S(1)}, f32[4,34,256]{2,1,0:T(8,128)S(1)}, u32[]{:S(2)}, u32[]{:S(2)}) collective-permute-start(f32[4,34,256]{2,1,0:T(8,128)S(1)} %get-tuple-element.79), channel_id=1, source_target_pairs={{8,16},{16,8},{9,17},{17,9},{10,18},{18,10},{11,19},{19,11},{12,20... | collective-permute-start | bytes 417800 | tf_op jit(solution)/shard_map/ppermute | solution.py:369
  11.6 3.2 %collective-permute-start.3 = (f32[6,34,256]{2,1,0:T(8,128)S(1)}, f32[6,34,256]{2,1,0:T(8,128)S(1)}, u32[]{:S(2)}, u32[]{:S(2)}) collective-permute-start(f32[6,34,256]{2,1,0:T(8,128)S(1)} %get-tuple-element.70), channel_id=1, source_target_pairs={{0,1},{1,0},{2,3},{3,2},{4,5},{5,4},{6,7},{7,6},{8,9},{9,8},{10,11... | collective-permute-start | bytes 626696 | tf_op jit(solution)/shard_map/ppermute | solution.py:368
  11.7 3.1 %collective-permute-start.2 = (f32[6,34,256]{2,1,0:T(8,128)S(1)}, f32[6,34,256]{2,1,0:T(8,128)S(1)}, u32[]{:S(2)}, u32[]{:S(2)}) collective-permute-start(f32[6,34,256]{2,1,0:T(8,128)S(1)} %get-tuple-element.71), channel_id=1, source_target_pairs={{1,2},{2,1},{3,4},{4,3},{5,6},{6,5},{9,10},{10,9},{11,12},{12,11},... | collective-permute-start | bytes 626696 | tf_op jit(solution)/shard_map/ppermute | solution.py:369
  16.2 9.2 %collective-permute-start.5 = (f32[4,32,256]{2,1,0:T(8,128)S(1)}, f32[4,32,256]{2,1,0:T(8,128)S(1)}, u32[]{:S(2)}, u32[]{:S(2)}) collective-permute-start(f32[4,32,256]{2,1,0:T(8,128)S(1)} %get-tuple-element.66), channel_id=1, source_target_pairs={{0,8},{8,0},{16,24},{24,16},{1,9},{9,1},{17,25},{25,17},{2,10},{10... | collective-permute-start | bytes 393224 | tf_op jit(solution)/shard_map/ppermute | solution.py:368
  22.4 3.0 %collective-permute-start.4 = (f32[4,32,256]{2,1,0:T(8,128)S(1)}, f32[4,32,256]{2,1,0:T(8,128)S(1)}, u32[]{:S(2)}, u32[]{:S(2)}) collective-permute-start(f32[4,32,256]{2,1,0:T(8,128)S(1)} %get-tuple-element.67), channel_id=1, source_target_pairs={{8,16},{16,8},{9,17},{17,9},{10,18},{18,10},{11,19},{19,11},{12,20... | collective-permute-start | bytes 393224 | tf_op jit(solution)/shard_map/ppermute | solution.py:369
  25.5 7.3 %collective-permute-start.7 = (f32[6,32,256]{2,1,0:T(8,128)S(1)}, f32[6,32,256]{2,1,0:T(8,128)S(1)}, u32[]{:S(2)}, u32[]{:S(2)}) collective-permute-start(f32[6,32,256]{2,1,0:T(8,128)S(1)} %get-tuple-element.74), channel_id=1, source_target_pairs={{0,1},{1,0},{2,3},{3,2},{4,5},{5,4},{6,7},{7,6},{8,9},{9,8},{10,11... | collective-permute-start | bytes 589832 | tf_op jit(solution)/shard_map/ppermute | solution.py:368
  30.4 2.4 %collective-permute-start.6 = (f32[6,32,256]{2,1,0:T(8,128)S(1)}, f32[6,32,256]{2,1,0:T(8,128)S(1)}, u32[]{:S(2)}, u32[]{:S(2)}) collective-permute-start(f32[6,32,256]{2,1,0:T(8,128)S(1)} %get-tuple-element.75), channel_id=1, source_target_pairs={{1,2},{2,1},{3,4},{4,3},{5,6},{6,5},{9,10},{10,9},{11,12},{12,11},... | collective-permute-start | bytes 589832 | tf_op jit(solution)/shard_map/ppermute | solution.py:369
